TPU v7x, 32 devices: a whole 2x2x4 slice. The times are simulated.
32 devices in a mesh: dp: 4 (over z), fsdp: 8 (over y, x, core).
Axes of the slice: x: 2, y: 2, z: 4, core: 2. Of those that a mesh axis runs over, the one named last changes fastest.
Arguments:
- tokens: bfloat16 [16384, 768], P(('dp', 'fsdp')), may hold values from -6 to 6
- condition: bfloat16 [64, 768], P(('dp', 'fsdp')), may hold values from -6 to 6
- ada_weight: bfloat16 [768, 4608], P('fsdp', 'dp'), may hold values from -0.21875 to 0.21875
- qkv_weight: bfloat16 [768, 2304], P('fsdp', 'dp'), may hold values from -0.21875 to 0.21875
- out_weight: bfloat16 [768, 768], P('fsdp', 'dp'), may hold values from -2 to 2
- shared_up: bfloat16 [768, 3072], P('fsdp', 'dp'), may hold values from -0.21875 to 0.21875
- shared_down: bfloat16 [3072, 768], P('fsdp', 'dp'), may hold values from -0.109375 to 0.109375
- router_weight: bfloat16 [768, 8], P('fsdp', 'dp'), may hold values from -0.21875 to 0.21875
- expert_up: bfloat16 [8, 768, 3072], P('dp', 'fsdp'), may hold values from -0.21875 to 0.21875
- expert_down: bfloat16 [8, 3072, 768], P('dp', 'fsdp'), may hold values from -0.109375 to 0.109375
- routes: int32 [16384, 2], P(('dp', 'fsdp')), may hold values from 0 to 7, all different within a row; in each aligned block of 512 rows (0 to 511, 512 to 1023, ...) at most 144 rows name the same one
- image_sizes: int32 [64], P(('dp', 'fsdp')), may hold values from 0 to 512, as said below
- cotangent: bfloat16 [16384, 768], P(('dp', 'fsdp')), may hold values from -6 to 6
Outputs:
- output: bfloat16 [16384, 768], P(('dp', 'fsdp'))
- tokens_grad: float32 [16384, 768], P(('dp', 'fsdp'))
- condition_grad: float32 [64, 768], P(('dp', 'fsdp'))
- ada_grad: float32 [768, 4608], P('fsdp', 'dp')
- qkv_grad: float32 [768, 2304], P('fsdp', 'dp')
- out_grad: float32 [768, 768], P('fsdp', 'dp')
- shared_up_grad: float32 [768, 3072], P('fsdp', 'dp')
- shared_down_grad: float32 [3072, 768], P('fsdp', 'dp')
- router_grad: float32 [768, 8], P('fsdp', 'dp')
- expert_up_grad: float32 [8, 768, 3072], P('dp', 'fsdp')
- expert_down_grad: float32 [8, 3072, 768], P('dp', 'fsdp')
- expert_counts: int32 [8], replicated
Inputs may be any that keep to these rules, and one draw needn't show every extreme that they name: `routes`: each row names two different experts; in the rows of one device no expert is named by more than 144 rows, and in every draw some expert is named by exactly 144 rows of some device. `image_sizes`: each aligned group of 2 entries is either one image of 512 patches followed by zeros, or k images of 256 patches followed by zeros, k from 1 to 2; in every draw some group holds one image of 512 and another holds 2 images of 256.
All inputs are finite; a program needn't handle non-finite values.
Results may differ from a plain program's by a relative error of at most 0.015.
The roundings to bfloat16 on the way count: a program that leaves them out, or rounds other values in their place, can miss the bound.
Values may be sent and summed in bfloat16 or wider, within the bound.
A program may use at most 512 MiB of HBM per device.

v0:
```python
import functools

import jax
import jax.numpy as jnp
from jax import lax
from jax.experimental import pallas as pl
from jax.experimental.pallas import tpu as pltpu
from jax.sharding import PartitionSpec as P

HEADS = 12
EXPERTS = 8
CAP = 144
IMG_DEV = 2
LONG = 512
MESH = pl.DeviceIdType.MESH


EXACT = lax.Precision.HIGHEST


def owners(image_sizes):
    starts = jnp.cumsum(image_sizes) - image_sizes
    position = jnp.arange(LONG, dtype=jnp.int32)[:, None]
    inside = (position >= starts[None, :]) & (position < (starts + image_sizes)[None, :])
    slot_ids = jnp.arange(IMG_DEV, dtype=jnp.int32)
    segment = jnp.sum(jnp.where(inside, slot_ids[None, :], 0), axis=1) + jnp.where(
        jnp.any(inside, axis=1), 0, IMG_DEV
    )
    return (inside.astype(jnp.float32), segment)


def dispatch_plan(routes):
    flat = routes.reshape(-1)
    onehot = (flat[:, None] == jnp.arange(EXPERTS, dtype=jnp.int32)[None, :]).astype(jnp.int32)
    before = jnp.cumsum(onehot, axis=0) - onehot
    position = jnp.sum(before * onehot, axis=1)
    target = flat * CAP + position
    assignment = jnp.arange(2 * LONG, dtype=jnp.int32)
    source = jnp.zeros((EXPERTS * CAP,), jnp.int32).at[target].set(assignment)
    filled = jnp.zeros((EXPERTS * CAP,), jnp.int32).at[target].set(1)
    return (target, source, filled)


def layer_norm(values_in):
    centred = values_in - jnp.mean(values_in, axis=-1, keepdims=True)
    inv_std = lax.rsqrt(jnp.mean(centred * centred, axis=-1, keepdims=True) + 1e-06)
    return (centred * inv_std, inv_std)


def norm_back(upstream, normed, inv_std):
    return (
        upstream
        - jnp.mean(upstream, axis=-1, keepdims=True)
        - normed * jnp.mean(upstream * normed, axis=-1, keepdims=True)
    ) * inv_std


def gelu_tanh(values_in):
    return jax.nn.gelu(values_in, approximate=True)


def gelu_back(values_in, upstream):
    return jax.vjp(gelu_tanh, values_in)[1](upstream)[0]


def collect(first, second, third):
    widened = (
        lax.all_gather(first, "dp", axis=1, tiled=True),
        lax.all_gather(second, "dp", axis=1, tiled=True),
        lax.all_gather(third, "dp", axis=1, tiled=True),
    )
    return (
        lax.all_gather(widened[0], "fsdp", axis=0, tiled=True),
        lax.all_gather(widened[1], "fsdp", axis=0, tiled=True),
        lax.all_gather(widened[2], "fsdp", axis=0, tiled=True),
    )


def spread(first, second, third):
    row_sums = (
        lax.psum_scatter(first, "fsdp", scatter_dimension=0, tiled=True),
        lax.psum_scatter(second, "fsdp", scatter_dimension=0, tiled=True),
        lax.psum_scatter(third, "fsdp", scatter_dimension=0, tiled=True),
    )
    return (
        lax.psum_scatter(row_sums[0], "dp", scatter_dimension=1, tiled=True),
        lax.psum_scatter(row_sums[1], "dp", scatter_dimension=1, tiled=True),
        lax.psum_scatter(row_sums[2], "dp", scatter_dimension=1, tiled=True),
    )


def gather_experts(up_shard, down_shard):
    return (
        lax.all_gather(up_shard, "fsdp", axis=1, tiled=True),
        lax.all_gather(down_shard, "fsdp", axis=1, tiled=True),
    )


def expert_forward(buffer_in, up_full, down_full):
    expert_pre = jnp.einsum(
        "secd,edf->secf", buffer_in, up_full, preferred_element_type=jnp.float32
    )
    expert_act = gelu_tanh(expert_pre).astype(jnp.bfloat16)
    expert_out = jnp.einsum(
        "secf,efd->secd", expert_act, down_full, preferred_element_type=jnp.float32
    ).astype(jnp.bfloat16)
    return (expert_pre, expert_act, expert_out)


def expert_backward(buffer_in, expert_pre, expert_act, d_out, up_full, down_full):
    d_act = jnp.einsum("secd,efd->secf", d_out, down_full, preferred_element_type=jnp.float32)
    d_pre = gelu_back(expert_pre, d_act).astype(jnp.bfloat16)
    d_rows = jnp.einsum(
        "secf,edf->secd", d_pre, up_full, preferred_element_type=jnp.float32
    ).astype(jnp.bfloat16)
    down_grad = jnp.einsum("secf,secd->efd", expert_act, d_out, preferred_element_type=jnp.float32)
    up_grad = jnp.einsum("secd,secf->edf", buffer_in, d_pre, preferred_element_type=jnp.float32)
    return (up_grad, down_grad, d_rows)


def attend(queries, keys_all, values_all, segment):
    row_count, head_count, head_size = queries.shape
    block_rows = min(512, row_count)
    block_count = row_count // block_rows
    score_scale = head_size ** (-0.5)

    def one_block(pieces):
        query_part, segment_part = pieces
        allowed = (segment_part[:, None] == segment[None, :])[None]
        scores = (
            jnp.einsum("qhd,khd->hqk", query_part, keys_all, preferred_element_type=jnp.float32)
            * score_scale
        )
        scores = jnp.where(allowed, scores, -1e30)
        row_max = jnp.max(scores, axis=-1, keepdims=True)
        weight = jnp.exp(scores - row_max)
        running = jnp.sum(weight, axis=-1, keepdims=True)
        probability = (weight / running).astype(jnp.bfloat16)
        attended = jnp.einsum(
            "hqk,khd->qhd", probability, values_all, preferred_element_type=jnp.float32
        )
        return (attended.astype(jnp.bfloat16), (row_max + jnp.log(running))[:, :, 0])

    return lax.map(
        one_block,
        (
            queries.reshape(block_count, block_rows, head_count, head_size),
            segment.reshape(block_count, block_rows),
        ),
    )


def attend_back(queries, keys_all, values_all, segment, log_totals, d_attended):
    row_count, head_count, head_size = queries.shape
    block_rows = min(512, row_count)
    block_count = row_count // block_rows
    score_scale = head_size ** (-0.5)

    def one_block(carry, pieces):
        key_sum, value_sum = carry
        query_part, segment_part, total_part, grad_part = pieces
        allowed = (segment_part[:, None] == segment[None, :])[None]
        scores = (
            jnp.einsum("qhd,khd->hqk", query_part, keys_all, preferred_element_type=jnp.float32)
            * score_scale
        )
        scores = jnp.where(allowed, scores, -1e30)
        probability = jnp.exp(scores - total_part[:, :, None])
        d_prob = jnp.einsum(
            "qhd,khd->hqk", grad_part, values_all, preferred_element_type=jnp.float32
        )
        d_scores = (
            probability * (d_prob - jnp.sum(probability * d_prob, axis=-1, keepdims=True))
        ).astype(jnp.bfloat16)
        query_grad = (
            jnp.einsum("hqk,khd->qhd", d_scores, keys_all, preferred_element_type=jnp.float32)
            * score_scale
        )
        key_sum = (
            key_sum
            + jnp.einsum("hqk,qhd->khd", d_scores, query_part, preferred_element_type=jnp.float32)
            * score_scale
        )
        value_sum = value_sum + jnp.einsum(
            "hqk,qhd->khd",
            probability.astype(jnp.bfloat16),
            grad_part,
            preferred_element_type=jnp.float32,
        )
        return ((key_sum, value_sum), query_grad)

    empty = jnp.zeros(keys_all.shape, jnp.float32)
    sums, query_grads = lax.scan(
        one_block,
        (empty, empty),
        (
            queries.reshape(block_count, block_rows, head_count, head_size),
            segment.reshape(block_count, block_rows),
            log_totals,
            d_attended.reshape(block_count, block_rows, head_count, head_size),
        ),
    )
    return (query_grads.reshape(row_count, head_count, head_size), sums[0], sums[1])


def shards(
    tokens,
    condition,
    ada_weight,
    qkv_weight,
    out_weight,
    shared_up,
    shared_down,
    router_weight,
    expert_up,
    expert_down,
    routes,
    image_sizes,
    cotangent,
):
    model_width = tokens.shape[1]
    head_size = model_width // HEADS
    inside, segment = owners(image_sizes)
    target, source, filled = dispatch_plan(routes)
    route_hot = (routes[:, :, None] == jnp.arange(EXPERTS, dtype=jnp.int32)[None, None, :]).astype(
        jnp.float32
    )
    live = (segment < IMG_DEV).astype(jnp.int32)
    local_counts = jnp.sum(live[:, None, None] * route_hot.astype(jnp.int32), axis=(0, 1))
    expert_counts = lax.psum(local_counts, ("dp", "fsdp"))
    ada_full, qkv_full, out_full = collect(ada_weight, qkv_weight, out_weight)
    cond_float = condition.astype(jnp.float32)
    activated = jax.nn.silu(cond_float).astype(jnp.bfloat16)
    modulation = jnp.dot(activated, ada_full, preferred_element_type=jnp.float32)
    per_row = jnp.dot(inside, modulation, precision=EXACT, preferred_element_type=jnp.float32)
    shift_one, scale_one, gate_one, shift_two, scale_two, gate_two = jnp.split(per_row, 6, axis=1)
    token_float = tokens.astype(jnp.float32)
    normed_one, inv_one = layer_norm(token_float)
    first_input = (normed_one * (1.0 + scale_one) + shift_one).astype(jnp.bfloat16)
    qkv_rows = jnp.dot(first_input, qkv_full, preferred_element_type=jnp.float32).astype(
        jnp.bfloat16
    )
    queries = qkv_rows[:, :model_width].reshape(-1, HEADS, head_size)
    keys_all = qkv_rows[:, model_width : 2 * model_width].reshape(-1, HEADS, head_size)
    values_all = qkv_rows[:, 2 * model_width :].reshape(-1, HEADS, head_size)
    attended_blocks, log_totals = attend(queries, keys_all, values_all, segment)
    attended = attended_blocks.reshape(-1, model_width)
    projected = jnp.dot(attended, out_full, preferred_element_type=jnp.float32)
    residual_one = token_float + gate_one * projected
    normed_two, inv_two = layer_norm(residual_one)
    second_input = (normed_two * (1.0 + scale_two) + shift_two).astype(jnp.bfloat16)
    shared_first, shared_second, router_full = collect(shared_up, shared_down, router_weight)
    shared_pre = jnp.dot(second_input, shared_first, preferred_element_type=jnp.float32)
    shared_act = gelu_tanh(shared_pre).astype(jnp.bfloat16)
    shared_out = jnp.dot(shared_act, shared_second, preferred_element_type=jnp.float32)
    logits = jnp.dot(second_input, router_full, preferred_element_type=jnp.float32)
    chosen = jnp.sum(logits[:, None, :] * route_hot, axis=-1)
    gate_share = jax.nn.softmax(chosen, axis=-1)
    buffer_rows = jnp.take(second_input, source // 2, axis=0).reshape(EXPERTS, CAP, model_width)
    up_full, down_full = gather_experts(expert_up, expert_down)
    groups = lax.axis_size("dp")
    expert_in = lax.all_to_all(
        buffer_rows.reshape(groups, EXPERTS // groups, CAP, model_width),
        "dp",
        split_axis=0,
        concat_axis=0,
        tiled=True,
    )
    expert_pre, expert_act, expert_out = expert_forward(expert_in, up_full, down_full)
    returned = lax.all_to_all(expert_out, "dp", split_axis=0, concat_axis=0, tiled=True).reshape(
        EXPERTS, CAP, model_width
    )
    picked = (
        jnp.take(returned.reshape(EXPERTS * CAP, model_width), target, axis=0)
        .reshape(-1, 2, model_width)
        .astype(jnp.float32)
    )
    mixed = shared_out + jnp.sum(gate_share[:, :, None] * picked, axis=1)
    output = (residual_one + gate_two * mixed).astype(jnp.bfloat16)
    upstream = cotangent.astype(jnp.float32)
    d_mixed = gate_two * upstream
    d_gate_two = upstream * mixed
    d_gate_share = jnp.sum(d_mixed[:, None, :] * picked, axis=-1)
    slot_gate = jnp.take(gate_share.reshape(-1), source) * filled.astype(jnp.float32)
    d_buffer = (
        (jnp.take(d_mixed, source // 2, axis=0) * slot_gate[:, None])
        .astype(jnp.bfloat16)
        .reshape(EXPERTS, CAP, model_width)
    )
    shared_first, shared_second, router_full = collect(shared_up, shared_down, router_weight)
    up_full, down_full = gather_experts(expert_up, expert_down)
    arrived = lax.all_to_all(
        d_buffer.reshape(groups, EXPERTS // groups, CAP, model_width),
        "dp",
        split_axis=0,
        concat_axis=0,
        tiled=True,
    )
    up_grad, down_grad, d_rows = expert_backward(
        expert_in, expert_pre, expert_act, arrived, up_full, down_full
    )
    d_returned = lax.all_to_all(d_rows, "dp", split_axis=0, concat_axis=0, tiled=True).reshape(
        EXPERTS, CAP, model_width
    )
    expert_sums = (
        lax.psum_scatter(up_grad, "fsdp", scatter_dimension=1, tiled=True),
        lax.psum_scatter(down_grad, "fsdp", scatter_dimension=1, tiled=True),
    )
    d_shared = d_mixed.astype(jnp.bfloat16)
    shared_second_grad = jnp.einsum(
        "tf,td->fd", shared_act, d_shared, preferred_element_type=jnp.float32
    )
    d_shared_act = jnp.einsum(
        "td,fd->tf", d_shared, shared_second, preferred_element_type=jnp.float32
    )
    d_shared_pre = gelu_back(shared_pre, d_shared_act).astype(jnp.bfloat16)
    shared_first_grad = jnp.einsum(
        "td,tf->df", second_input, d_shared_pre, preferred_element_type=jnp.float32
    )
    d_chosen = gate_share * (
        d_gate_share - jnp.sum(gate_share * d_gate_share, axis=-1, keepdims=True)
    )
    d_logits = jnp.sum(d_chosen[:, :, None] * route_hot, axis=1).astype(jnp.bfloat16)
    router_grad = jnp.einsum(
        "td,te->de", second_input, d_logits, preferred_element_type=jnp.float32
    )
    from_experts = (
        jnp.take(d_returned.reshape(EXPERTS * CAP, model_width), target, axis=0)
        .reshape(-1, 2, model_width)
        .astype(jnp.float32)
    )
    d_second = (
        jnp.einsum("tf,df->td", d_shared_pre, shared_first, preferred_element_type=jnp.float32)
        + jnp.einsum("te,de->td", d_logits, router_full, preferred_element_type=jnp.float32)
        + jnp.sum(from_experts, axis=1)
    )
    mlp_sums = spread(shared_first_grad, shared_second_grad, router_grad)
    d_scale_two = d_second * normed_two
    d_residual = upstream + norm_back(d_second * (1.0 + scale_two), normed_two, inv_two)
    ada_full, qkv_full, out_full = collect(ada_weight, qkv_weight, out_weight)
    d_projected = (gate_one * d_residual).astype(jnp.bfloat16)
    d_gate_one = d_residual * projected
    out_grad = jnp.einsum("td,te->de", attended, d_projected, preferred_element_type=jnp.float32)
    d_attended = jnp.einsum(
        "te,de->td", d_projected, out_full, preferred_element_type=jnp.float32
    ).astype(jnp.bfloat16)
    d_queries, d_keys, d_values = attend_back(
        queries, keys_all, values_all, segment, log_totals, d_attended.reshape(-1, HEADS, head_size)
    )
    d_qkv = jnp.concatenate(
        [
            d_queries.reshape(-1, model_width),
            d_keys.reshape(-1, model_width),
            d_values.reshape(-1, model_width),
        ],
        axis=1,
    ).astype(jnp.bfloat16)
    qkv_grad = jnp.einsum("td,te->de", first_input, d_qkv, preferred_element_type=jnp.float32)
    d_first = jnp.einsum("te,de->td", d_qkv, qkv_full, preferred_element_type=jnp.float32)
    d_scale_one = d_first * normed_one
    tokens_grad = d_residual + norm_back(d_first * (1.0 + scale_one), normed_one, inv_one)
    d_per_row = jnp.concatenate(
        [d_first, d_scale_one, d_gate_one, d_second, d_scale_two, d_gate_two], axis=1
    )
    d_modulation = jnp.einsum(
        "tj,te->je", inside, d_per_row, precision=EXACT, preferred_element_type=jnp.float32
    ).astype(jnp.bfloat16)
    ada_grad = jnp.einsum("jd,je->de", activated, d_modulation, preferred_element_type=jnp.float32)
    d_activated = jnp.einsum(
        "je,de->jd", d_modulation, ada_full, preferred_element_type=jnp.float32
    )
    condition_grad = jax.vjp(jax.nn.silu, cond_float)[1](d_activated)[0]
    attn_sums = spread(ada_grad, qkv_grad, out_grad)
    return (
        output,
        tokens_grad,
        condition_grad,
        attn_sums[0],
        attn_sums[1],
        attn_sums[2],
        mlp_sums[0],
        mlp_sums[1],
        mlp_sums[2],
        expert_sums[0],
        expert_sums[1],
        expert_counts,
    )


def at(d, s, c):
    return (d, 2 * s + c)


def slot(kind, f, d):
    if kind == "cols":
        return (pl.ds(pl.multiple_of(96 * f, 96), 96), pl.ds(pl.multiple_of(768 * d, 768), 768))
    return (pl.ds(pl.multiple_of(192 * d, 192), 192), pl.ds(pl.multiple_of(384 * f, 384), 384))


def half_slot(kind, f, d, h):
    if kind == "cols":
        return (
            pl.ds(pl.multiple_of(96 * f, 96), 96),
            pl.ds(pl.multiple_of(768 * d + 384 * h, 384), 384),
        )
    return (
        pl.ds(pl.multiple_of(192 * d + 96 * h, 96), 96),
        pl.ds(pl.multiple_of(384 * f, 384), 384),
    )


def place():
    d = lax.axis_index("dp")
    f = lax.axis_index("fsdp")
    return d, f // 2, lax.rem(f, 2)


def flip(v, bit):
    return v + bit - 2 * bit * lax.rem(v // bit, 2)


def greet(devices):
    barrier = pltpu.get_barrier_semaphore()
    for device in devices:
        pl.semaphore_signal(barrier, inc=1, device_id=device, device_id_type=MESH)
    pl.semaphore_wait(barrier, len(devices))


def push(src, dst, send_sem, recv_sem, device):
    return pltpu.make_async_remote_copy(
        src_ref=src,
        dst_ref=dst,
        send_sem=send_sem,
        recv_sem=recv_sem,
        device_id=device,
        device_id_type=MESH,
    )


GATHER_SEMS = 3 + 8 + 8 + 20


class Gather:
    def __init__(self, kind, shard, full, ssem, rsem, lsem):
        self.kind, self.shard, self.full = kind, shard, full
        self.ssem, self.rsem, self.lsem = ssem, rsem, lsem
        self.d, self.s, self.c = place()
        self.sent = []

    def f(self, s):
        return 2 * s + self.c

    def go(self, index, where, device, src=None):
        ref = self.full.at[where]
        copy = push(
            ref if src is None else src, ref, self.ssem.at[index], self.rsem.at[index], device
        )
        copy.start()
        self.sent.append(copy)

    def arrived(self, index, where):
        ref = self.full.at[where]
        push(ref, ref, self.ssem.at[index], self.rsem.at[index], at(self.d, self.s, self.c)).wait_recv()

    def start(self):
        d, s, c = self.d, self.s, self.c
        mine = slot(self.kind, self.f(s), d)
        self.own = pltpu.make_async_copy(self.shard, self.full.at[mine], self.lsem)
        self.own.start()
        self.go(1, mine, at(flip(d, 2), s, c), self.shard)
        self.go(0, mine, at(flip(d, 1), s, c), self.shard)
        self.go(3, mine, at(d, flip(s, 1), c), self.shard)
        self.go(4, mine, at(d, flip(s, 2), c), self.shard)
        self.go(19, mine, at(d, s, 1 - c), self.shard)

    def source(self, k):
        return (self.d, flip(self.d, 1), flip(self.d, 2), flip(flip(self.d, 1), 2))[k]

    def spread_z(self, k):
        d, s, c = self.d, self.s, self.c
        block = slot(self.kind, self.f(s), self.source(k))
        self.arrived(k - 1, block)
        if k == 2:
            self.go(2, block, at(flip(d, 1), s, c))
        self.go(3 + 2 * k, block, at(d, flip(s, 1), c))
        self.go(4 + 2 * k, block, at(d, flip(s, 2), c))
        self.go(19 + 5 * k, block, at(d, s, 1 - c))

    def relay(self, k):
        d, s, c = self.d, self.s, self.c
        source = self.source(k)
        sx, sy = flip(s, 1), flip(s, 2)
        from_x = slot(self.kind, self.f(sx), source)
        from_y = slot(self.kind, self.f(sy), source)
        self.arrived(3 + 2 * k, from_x)
        self.go(11 + 2 * k, half_slot(self.kind, self.f(sx), source, 0), at(d, sy, c))
        self.go(20 + 5 * k, from_x, at(d, s, 1 - c))
        self.arrived(4 + 2 * k, from_y)
        self.go(12 + 2 * k, half_slot(self.kind, self.f(sy), source, 1), at(d, sx, c))
        self.go(21 + 5 * k, from_y, at(d, s, 1 - c))

    def corner(self, k):
        d, s, c = self.d, self.s, self.c
        source = self.source(k)
        sd = flip(flip(s, 1), 2)
        for h in range(2):
            where = half_slot(self.kind, self.f(sd), source, h)
            self.arrived(11 + 2 * k + h, where)
            self.go(22 + 5 * k + h, where, at(d, s, 1 - c))

    def finish(self):
        d, s, c = self.d, self.s, self.c
        sx, sy = flip(s, 1), flip(s, 2)
        sd = flip(sx, 2)
        self.own.wait()
        for k in range(4):
            source = self.source(k)
            for j, position in enumerate((s, sx, sy)):
                self.arrived(19 + 5 * k + j, slot(self.kind, 2 * position + 1 - c, source))
            for h in range(2):
                self.arrived(22 + 5 * k + h, half_slot(self.kind, 2 * sd + 1 - c, source, h))
        for copy in self.sent:
            copy.wait_send()


class Line:
    def __init__(self, kind, shard, line, ssem, rsem, lsem):
        self.kind, self.shard, self.line = kind, shard, line
        self.ssem, self.rsem, self.lsem = ssem, rsem, lsem
        self.d, self.s, self.c = place()

    def block(self, d):
        if self.kind == "cols":
            return self.line.at[:, pl.ds(pl.multiple_of(768 * d, 768), 768)]
        return self.line.at[pl.ds(pl.multiple_of(192 * d, 192), 192)]

    def copy(self, index, src, source, target):
        return push(
            src, self.block(source), self.ssem.at[index], self.rsem.at[index], at(target, self.s, self.c)
        )

    def start(self):
        d = self.d
        self.own = pltpu.make_async_copy(self.shard, self.block(d), self.lsem)
        self.own.start()
        self.sent = [
            self.copy(0, self.shard, d, flip(d, 2)),
            self.copy(1, self.shard, d, flip(d, 1)),
        ]
        for copy in self.sent:
            copy.start()

    def relay(self):
        d2 = flip(self.d, 2)
        self.copy(0, self.shard, d2, d2).wait_recv()
        copy = self.copy(2, self.block(d2), d2, flip(self.d, 1))
        copy.start()
        self.sent.append(copy)

    def finish(self):
        d1 = flip(self.d, 1)
        self.own.wait()
        self.copy(1, self.shard, d1, d1).wait_recv()
        self.copy(2, self.shard, flip(d1, 2), d1).wait_recv()
        for copy in self.sent:
            copy.wait_send()


class Spread:
    def __init__(self, kind, line, full, ssem, rsem, lsem):
        self.kind, self.line, self.full = kind, line, full
        self.ssem, self.rsem, self.lsem = ssem, rsem, lsem
        self.d, self.s, self.c = place()
        self.sx, self.sy = flip(self.s, 1), flip(self.s, 2)
        self.sd = flip(self.sx, 2)
        self.mate = at(self.d, self.s, 1 - self.c)
        self.to_x, self.to_y = at(self.d, self.sx, self.c), at(self.d, self.sy, self.c)
        self.sent = []

    def block(self, position, c, h=None):
        f = 2 * position + c
        if self.kind == "cols":
            rows = pl.ds(pl.multiple_of(96 * f, 96), 96)
            return self.full.at[rows] if h is None else self.full.at[rows, pl.ds(1536 * h, 1536)]
        columns = pl.ds(pl.multiple_of(384 * f, 384), 384)
        rows = pl.ds(0, 768) if h is None else pl.ds(384 * h, 384)
        return self.full.at[rows, columns]

    def go(self, index, ref, device, src=None):
        copy = push(
            ref if src is None else src, ref, self.ssem.at[index], self.rsem.at[index], device
        )
        copy.start()
        self.sent.append(copy)

    def arrived(self, index, ref):
        push(ref, ref, self.ssem.at[index], self.rsem.at[index], self.mate).wait_recv()

    def start(self):
        mine = self.block(self.s, self.c)
        self.own = pltpu.make_async_copy(self.line, mine, self.lsem)
        self.own.start()
        self.go(0, mine, self.to_x, self.line)
        self.go(1, mine, self.to_y, self.line)
        self.go(2, mine, self.mate, self.line)

    def relay(self):
        c = self.c
        from_x, from_y = self.block(self.sx, c), self.block(self.sy, c)
        self.arrived(0, from_x)
        self.go(3, self.block(self.sx, c, 0), self.to_y)
        self.go(5, from_x, self.mate)
        self.arrived(1, from_y)
        self.go(4, self.block(self.sy, c, 1), self.to_x)
        self.go(6, from_y, self.mate)

    def corner(self):
        for h in range(2):
            ref = self.block(self.sd, self.c, h)
            self.arrived(3 + h, ref)
            self.go(7 + h, ref, self.mate)

    def finish(self):
        c = 1 - self.c
        self.own.wait()
        self.arrived(2, self.block(self.s, c))
        self.arrived(5, self.block(self.sx, c))
        self.arrived(6, self.block(self.sy, c))
        for h in range(2):
            self.arrived(7 + h, self.block(self.sd, c, h))
        for copy in self.sent:
            copy.wait_send()


class Near:
    def __init__(self, up_shard, down_shard, up_mate, up_x, up_y, down_own, down_mate, ssem, rsem, lsem):
        d, s, c = place()
        self.local = pltpu.make_async_copy(down_shard.at[c], down_own, lsem)
        plan = (
            (up_shard, c, up_x, flip(s, 1)),
            (up_shard, c, up_y, flip(s, 2)),
            (up_shard, 1 - c, up_mate, s),
            (down_shard, 1 - c, down_mate, s),
        )
        self.away = [
            push(shard.at[which], out, ssem.at[i], rsem.at[i], at(d, position, which))
            for i, (shard, which, out, position) in enumerate(plan)
        ]

    def start(self):
        for copy in self.away + [self.local]:
            copy.start()

    def finish(self):
        for copy in self.away + [self.local]:
            copy.wait()


class Pair:
    def __init__(self, over_x, into_x, over_y, into_y, ssem, rsem):
        d, s, c = place()
        self.copies = [
            push(over_x, into_x, ssem.at[0], rsem.at[0], at(d, flip(s, 1), c)),
            push(over_y, into_y, ssem.at[1], rsem.at[1], at(d, flip(s, 2), c)),
        ]

    def start(self):
        for copy in self.copies:
            copy.start()

    def finish(self):
        for copy in self.copies:
            copy.wait()


def everyone_else():
    me = lax.axis_index("dp") * 8 + lax.axis_index("fsdp")

    def other(k):
        device = lax.rem(me + k, 32)
        return (device // 8, lax.rem(device, 8))

    return me, other


def open_kernel(
    shard, router, act_ref, ada_ref, up_shard, down_shard, expert_up, expert_down,
    full, routers, seen, rows_out, up_line, down_line, up_mate, up_x, up_y, down_own, down_mate,
    heard, part, got, mixed, ssem, rsem, lsem, asem, brsem, rssem, rrsem, tssem, trsem, zssem, zrsem,
    us, ur, ds, dr, es, er, el,
):
    me, other = everyone_else()
    d, s, c = place()
    f = 2 * s + c
    barrier = pltpu.get_barrier_semaphore()

    def hello(k, carry):
        pl.semaphore_signal(barrier, inc=1, device_id=other(k), device_id_type=MESH)
        return carry

    lax.fori_loop(1, 32, hello, 0)
    pl.semaphore_wait(barrier, 31)

    def act_copy(k, source):
        device = other(k)
        return push(act_ref.at[device[1]], heard.at[source], asem.at[k], brsem.at[k], device)

    def router_copy(k, source):
        return push(router, routers.at[source], rssem.at[k], rrsem.at[k], other(k))

    def send(k, carry):
        act_copy(k, me).start()
        return carry

    lax.fori_loop(1, 32, send, 0)
    gather = Gather("cols", shard, full, ssem, rsem, lsem.at[0])
    gather.start()
    near = Near(
        expert_up, expert_down, up_mate, up_x, up_y, down_own, down_mate, es, er, el.at[0]
    )
    near.start()
    lines = (
        Line("cols", up_shard, up_line, us, ur, lsem.at[3]),
        Line("rows", down_shard, down_line, ds, dr, lsem.at[4]),
    )
    own_router = pltpu.make_async_copy(router, routers.at[me], lsem.at[1])
    own_router.start()

    def send_router(k, carry):
        router_copy(k, me).start()
        return carry

    lax.fori_loop(1, 32, send_router, 0)
    heard[me] = act_ref[f]

    def take(k, carry):
        copy = act_copy(k, lax.rem(me + 32 - k, 32))
        copy.wait_recv()
        return carry

    lax.fori_loop(1, 32, take, 0)
    everything = heard[...].reshape(256, 128)
    row = lax.broadcasted_iota(jnp.int32, (64, 256), 0)
    column = lax.broadcasted_iota(jnp.int32, (64, 256), 1)
    source = lax.rem(row // 2, 4) * 8 + row // 8
    pick = (column == source * 8 + lax.rem(row, 2)).astype(jnp.bfloat16)
    compact = jnp.dot(
        pick, everything.astype(jnp.bfloat16), preferred_element_type=jnp.float32
    ).astype(jnp.bfloat16)
    seen[...] = jnp.concatenate(
        [compact.astype(jnp.float32), jnp.sum(heard[...], axis=0)], axis=0
    )
    part[...] = jnp.dot(compact, ada_ref[...], preferred_element_type=jnp.float32).reshape(
        8, 8, 1152
    )

    def tile_copy(k):
        target = lax.rem(f + k, 8)
        return push(part.at[target], got.at[k], tssem.at[k], trsem.at[k], (d, target))

    for k in range(1, 8):
        tile_copy(k).start()
    gather.spread_z(1)
    gather.spread_z(2)
    gather.relay(0)
    for k in range(1, 8):
        tile_copy(k).wait_recv()
    total = part[f]
    for k in range(1, 8):
        total = total + got[k]
    mixed[...] = total
    zs = []
    for k in range(1, 4):
        copy = push(mixed, rows_out.at[d], zssem.at[k], zrsem.at[k], at(lax.rem(d + k, 4), s, c))
        copy.start()
        zs.append(copy)
    own_rows = pltpu.make_async_copy(mixed, rows_out.at[d], lsem.at[2])
    own_rows.start()
    gather.spread_z(3)
    for line in lines:
        line.start()
    gather.relay(1)
    gather.corner(0)
    gather.relay(2)
    gather.corner(1)
    gather.relay(3)
    gather.corner(2)
    for line in lines:
        line.relay()
    gather.corner(3)
    gather.finish()
    for line in lines:
        line.finish()
    near.finish()
    own_router.wait()
    own_rows.wait()
    for k in range(1, 4):
        push(
            mixed, rows_out.at[lax.rem(d + 4 - k, 4)], zssem.at[k], zrsem.at[k],
            at(lax.rem(d + k, 4), s, c),
        ).wait_recv()
    for copy in zs:
        copy.wait_send()
    for k in range(1, 8):
        tile_copy(k).wait_send()

    def drain(k, carry):
        act_copy(k, me).wait_send()
        copy = router_copy(k, lax.rem(me + 32 - k, 32))
        copy.wait_recv()
        copy.wait_send()
        return carry

    lax.fori_loop(1, 32, drain, 0)


DMA = pltpu.SemaphoreType.DMA
ANYWHERE = pl.BlockSpec(memory_space=pl.ANY)
ONCHIP = pl.BlockSpec(memory_space=pltpu.VMEM)


def opening(shard, router, act, ada, up_shard, down_shard, expert_up, expert_down):
    return pl.pallas_call(
        open_kernel,
        out_shape=(
            jax.ShapeDtypeStruct((768, 3072), jnp.bfloat16),
            jax.ShapeDtypeStruct((32, 16, 128), jnp.bfloat16),
            jax.ShapeDtypeStruct((72, 128), jnp.float32),
            jax.ShapeDtypeStruct((4, 8, 1152), jnp.float32),
            jax.ShapeDtypeStruct((96, 3072), jnp.bfloat16),
            jax.ShapeDtypeStruct((768, 384), jnp.bfloat16),
        )
        + (jax.ShapeDtypeStruct((96, 3072), jnp.bfloat16),) * 3
        + (jax.ShapeDtypeStruct((384, 768), jnp.bfloat16),) * 2,
        in_specs=[ONCHIP] * 6 + [ANYWHERE] * 2,
        out_specs=(ANYWHERE, ANYWHERE, ONCHIP) + (ANYWHERE,) * 8,
        scratch_shapes=[
            pltpu.VMEM((32, 8, 128), jnp.float32),
            pltpu.VMEM((8, 8, 1152), jnp.float32),
            pltpu.VMEM((8, 8, 1152), jnp.float32),
            pltpu.VMEM((8, 1152), jnp.float32),
            DMA((GATHER_SEMS,)), DMA((GATHER_SEMS,)), DMA((5,)),
            DMA((32,)), DMA((32,)), DMA((32,)), DMA((32,)),
            DMA((8,)), DMA((8,)), DMA((4,)), DMA((4,)),
            DMA((3,)), DMA((3,)), DMA((3,)), DMA((3,)),
            DMA((4,)), DMA((4,)), DMA((1,)),
        ],
        compiler_params=pltpu.CompilerParams(collective_id=0, has_side_effects=True),
        name="opening",
    )(shard, router, act, ada, up_shard, down_shard, expert_up, expert_down)


def group_of(d, s, c):
    return [(j, at(lax.rem(d + j // 2, 4), s, lax.rem(c + j, 2))) for j in range(1, 8)]


class Swap:
    def __init__(self, blocks, out, ssem, rsem, lsem):
        self.blocks, self.out, self.ssem, self.rsem, self.lsem = blocks, out, ssem, rsem, lsem
        self.d, self.s, self.c = place()
        self.me = 2 * self.d + self.c

    def copy(self, j, landing):
        target_d = lax.rem(self.d + j // 2, 4)
        target_c = lax.rem(self.c + j, 2)
        return push(
            self.blocks.at[2 * target_d + target_c],
            self.out.at[landing],
            self.ssem.at[j],
            self.rsem.at[j],
            at(target_d, self.s, target_c),
        )

    def start(self):
        for j in (4, 5, 2, 3, 6, 7, 1):
            self.copy(j, self.me).start()
        self.own = pltpu.make_async_copy(
            self.blocks.at[self.me], self.out.at[self.me], self.lsem
        )
        self.own.start()

    def send(self, step):
        for j in (2 * step, 2 * step + 1):
            if j:
                self.copy(j, self.me).start()
            else:
                self.own = pltpu.make_async_copy(
                    self.blocks.at[self.me], self.out.at[self.me], self.lsem
                )
                self.own.start()

    def finish(self):
        self.own.wait()
        for j in range(1, 8):
            source_d = lax.rem(self.d + 4 - j // 2, 4)
            source_c = lax.rem(self.c + j, 2)
            copy = self.copy(j, 2 * source_d + source_c)
            copy.wait_recv()
            copy.wait_send()


def nt(left, right):
    return lax.dot_general(left, right, (((1,), (1,)), ((), ())), preferred_element_type=jnp.float32)


def tn(left, right):
    return lax.dot_general(left, right, (((0,), (0,)), ((), ())), preferred_element_type=jnp.float32)


def nn(left, right):
    return jnp.dot(left, right, preferred_element_type=jnp.float32)


GELU_SCALE = 0.7978845608028654


def gelu_pair(v):
    square = v * v
    bend = jnp.tanh(GELU_SCALE * (v + 0.044715 * (square * v)))
    half = 0.5 * (1.0 + bend)
    slope = half + 0.5 * v * (1.0 - bend * bend) * (
        GELU_SCALE * (1.0 + (3.0 * 0.044715) * square)
    )
    return v * half, slope


HIDDEN = 512


def out_kernel(
    rows, grads, up_line, down_line, tokens, d_tokens, up_x, up_y, down_mate, down_x,
    rows_in, grads_in, up_corner, down_x_mate, down_y_mate, down_corner, mixed_out, d_tokens_out, up_grad, down_grad,
    up_full, down_full, tokens_t, d_tokens_t, s1, r1, s2, r2, ssem, rsem, ssem2, rsem2, lsem,
    es, er, fs, fr, gs, gr,
):
    d, s, c = place()
    greet([device for _, device in group_of(d, s, c)] + [at(d, flip(s, 1), c), at(d, flip(s, 2), c)])
    both = (
        Spread("cols", up_line, up_full, ssem, rsem, lsem.at[0]),
        Spread("rows", down_line, down_full, ssem2, rsem2, lsem.at[1]),
    )
    swap_a = Swap(rows, rows_in, s1, r1, lsem.at[2])
    swap_b = Swap(grads, grads_in, s2, r2, lsem.at[3])
    for g in both:
        g.start()
    swap_a.start()
    swap_b.start()
    mates = Pair(down_mate, down_x_mate, down_mate, down_y_mate, gs, gr)
    up_corners = Pair(up_y, up_corner.at[1], up_x, up_corner.at[0], es, er)
    down_corners = Pair(down_y_mate, down_corner.at[1], down_x, down_corner.at[0], fs, fr)
    tokens_t[...] = tokens[...].T
    d_tokens_t[...] = d_tokens[...].T
    mixed_out[...] = jnp.zeros_like(mixed_out)
    d_tokens_out[...] = jnp.zeros_like(d_tokens_out)
    for g in both:
        g.relay()
    mates.start()
    up_corners.start()
    for g in both:
        g.corner()
    for g in both:
        g.finish()

    def block(b, carry):
        where = pl.ds(pl.multiple_of(b * HIDDEN, HIDDEN), HIDDEN)
        up, down = up_full[:, where], down_full[:, where]
        act, slope = gelu_pair(nn(tokens[...], up))
        act = act.astype(jnp.bfloat16)
        mixed_out[...] += nt(act, down)
        down_grad[:, where] = nn(d_tokens_t[...], act).astype(jnp.bfloat16)
        d_pre = (slope * nn(d_tokens[...], down)).astype(jnp.bfloat16)
        d_tokens_out[...] += nt(d_pre, up)
        up_grad[:, where] = nn(tokens_t[...], d_pre).astype(jnp.bfloat16)
        return carry

    lax.fori_loop(0, 1, block, 0)
    mates.finish()
    down_corners.start()
    lax.fori_loop(1, 3072 // HIDDEN, block, 0)
    swap_a.finish()
    swap_b.finish()
    up_corners.finish()
    down_corners.finish()


def outbound(*operands):
    bf, f32 = jnp.bfloat16, jnp.float32
    return pl.pallas_call(
        out_kernel,
        out_shape=(
            jax.ShapeDtypeStruct((8, 144, 768), bf),
            jax.ShapeDtypeStruct((8, 144, 768), bf),
            jax.ShapeDtypeStruct((2, 96, 3072), bf),
            jax.ShapeDtypeStruct((384, 768), bf),
            jax.ShapeDtypeStruct((384, 768), bf),
            jax.ShapeDtypeStruct((2, 384, 768), bf),
            jax.ShapeDtypeStruct((512, 768), f32),
            jax.ShapeDtypeStruct((512, 768), f32),
            jax.ShapeDtypeStruct((768, 3072), bf),
            jax.ShapeDtypeStruct((768, 3072), bf),
        ),
        in_specs=[ONCHIP] * 6 + [ANYWHERE] * 4,
        out_specs=(ANYWHERE,) * 6 + (ONCHIP,) * 4,
        scratch_shapes=[pltpu.VMEM((768, 3072), bf)] * 2
        + [pltpu.VMEM((768, 512), bf)] * 2
        + [DMA((8,))] * 4
        + [DMA((9,))] * 4
        + [DMA((4,))]
        + [DMA((2,))] * 6,
        compiler_params=pltpu.CompilerParams(
            collective_id=1, has_side_effects=True, vmem_limit_bytes=60 << 20
        ),
        name="outbound",
    )(*operands)


def widened(ref):
    return ref[...].astype(jnp.float32)


class Parts:
    def __init__(self, grad, keep, over_x, over_y, sem, rsem=None):
        d, s, c = place()
        sx, sy = flip(s, 1), flip(s, 2)
        sd = flip(sx, 2)
        rows = grad.shape[0] // 8
        slots = (
            (s, 0, keep.at[0, 0], s), (sy, 0, keep.at[0, 1], s),
            (s, 1, keep.at[1, 0], s), (sx, 1, keep.at[1, 1], s),
            (sx, 0, over_x.at[0], sx), (sd, 0, over_x.at[1], sx),
            (sy, 1, over_y.at[0], sy), (sd, 1, over_y.at[1], sy),
        )
        self.copies, self.away = [], []
        for i, (position, h, out, target) in enumerate(slots):
            part = grad.at[pl.ds(pl.multiple_of((2 * position + h) * rows, 32), rows)]
            if i < 4 or rsem is None:
                self.copies.append(pltpu.make_async_copy(part, out, sem.at[i]))
            else:
                self.away.append(push(part, out, sem.at[i], rsem.at[i], at(d, target, c)))

    def start(self):
        for copy in self.away + self.copies:
            copy.start()

    def finish(self):
        for copy in self.copies + self.away:
            copy.wait()


class Pieces:
    def __init__(self, parts, full, sem):
        d, s, c = place()
        rows = full.shape[0] // 8
        sx, sy = flip(s, 1), flip(s, 2)
        positions = [p for p in (s, sx, sy, flip(sx, 2)) for _ in range(2)]
        self.copies = [
            pltpu.make_async_copy(
                part,
                full.at[pl.ds(pl.multiple_of(rows * (2 * p + (c if i % 2 == 0 else 1 - c)), 32), rows)],
                sem.at[i],
            )
            for i, (p, part) in enumerate(zip(positions, parts))
        ]

    def start(self):
        for copy in self.copies:
            copy.start()

    def finish(self):
        for copy in self.copies:
            copy.wait()


def expert_kernel(
    rows, grads, expert_up, up_m, up_x0, up_x1, up_y0, up_y1, up_corner,
    down_own, down_m, down_x0, down_x1, down_y0, down_y1, down_corner, first_grad, second_grad,
    rows_back, grads_back, up_keep, up_x, up_y, down_keep, down_x, down_y, first_part, second_part,
    up, down, act, d_pre, made, d_made, total, d_total, up_grad, down_grad, rows_t,
    fo, fm, fn, ff, fs, fr, fl, so, sm, sn, sf, ss, sr, sl,
    s1, r1, s2, r2, lsem, wsem, vsem, psem, arsem, qsem,
):
    bf = jnp.bfloat16
    d, s, c = place()
    weights = (
        Pieces(
            (expert_up.at[c], up_m, up_x0, up_x1, up_y0, up_y1, up_corner.at[0], up_corner.at[1]), up, wsem
        ),
        Pieces(
            (down_own, down_m, down_x0, down_x1, down_y0, down_y1, down_corner.at[0], down_corner.at[1]),
            down, vsem,
        ),
    )
    for each in weights:
        each.start()
    greet([device for _, device in group_of(d, s, c)] + [at(d, flip(s, 1), c), at(d, flip(s, 2), c)])
    sums = (
        DenseSum("cols", first_grad, first_part, fo, fm, fn, ff, None, fs, fr, fl),
        DenseSum("rows", second_grad, second_part, so, sm, sn, sf, None, ss, sr, sl),
    )
    for each in sums:
        each.start()
    swap_a = Swap(made, rows_back, s1, r1, lsem.at[0])
    swap_b = Swap(d_made, grads_back, s2, r2, lsem.at[1])
    for each in weights:
        each.finish()
    for step in (2, 1, 3, 0):
        there = lax.rem(d + step, 4)
        chunk = pl.ds(2 * there, 2)
        lines = pl.ds(pl.multiple_of(288 * there, 288), 288)
        x = rows[chunk].reshape(288, 768)
        g = grads[chunk].reshape(288, 768)
        total[...] = jnp.zeros_like(total)
        d_total[...] = jnp.zeros_like(d_total)

        def block(b, carry):
            where = pl.ds(pl.multiple_of(b * HIDDEN, HIDDEN), HIDDEN)
            up_part, down_part = up[:, where], down[where]
            made_act, slope = gelu_pair(nn(x, up_part))
            made_act = made_act.astype(bf)
            act[lines, where] = made_act
            total[...] += nn(made_act, down_part)
            d_part = (slope * nt(g, down_part)).astype(bf)
            d_pre[lines, where] = d_part
            d_total[...] += nt(d_part, up_part)
            return carry

        lax.fori_loop(0, 3072 // HIDDEN, block, 0)
        made[chunk] = total[...].astype(bf).reshape(2, 144, 768)
        d_made[chunk] = d_total[...].astype(bf).reshape(2, 144, 768)
        swap_a.send(step)
        swap_b.send(step)
        if step == 2:
            for each in sums:
                each.merge()
        if step == 3:
            for each in sums:
                each.join()
    rows_t[...] = rows.reshape(1152, 768)[...].T
    g_all = grads.reshape(1152, 768)

    def up_block(b, carry):
        where = pl.ds(pl.multiple_of(b * HIDDEN, HIDDEN), HIDDEN)
        up_grad[:, where] = nn(rows_t[...], d_pre[:, where]).astype(bf)
        return carry

    def down_block(b, carry):
        where = pl.ds(pl.multiple_of(384 * b, 384), 384)
        down_grad[where] = tn(act[:, where], g_all[...]).astype(bf)
        return carry

    up_parts = Parts(up_grad, up_keep, up_x, up_y, psem, arsem)
    down_parts = Parts(down_grad, down_keep, down_x, down_y, qsem)
    lax.fori_loop(0, 3072 // HIDDEN, up_block, 0)
    up_parts.start()
    lax.fori_loop(0, 8, down_block, 0)
    down_parts.start()
    for each in sums:
        each.close()
    swap_a.finish()
    swap_b.finish()
    up_parts.finish()
    down_parts.finish()


def experts(rows, grads, up_pieces, down_pieces, first_grad, second_grad):
    bf, f32 = jnp.bfloat16, jnp.float32

    def rooms(piece, half):
        return [
            pltpu.VMEM((4,) + piece, bf),
            pltpu.VMEM((4,) + piece, bf),
            pltpu.VMEM((2,) + half, bf),
            pltpu.VMEM((2,) + piece, bf),
            DMA((8,)),
            DMA((8,)),
            DMA((4,)),
        ]

    def parts(r, n):
        return (
            jax.ShapeDtypeStruct((2, 2, r, n), bf),
            jax.ShapeDtypeStruct((2, r, n), bf),
            jax.ShapeDtypeStruct((2, r, n), bf),
        )

    return pl.pallas_call(
        expert_kernel,
        out_shape=(
            jax.ShapeDtypeStruct((8, 144, 768), bf),
            jax.ShapeDtypeStruct((8, 144, 768), bf),
        )
        + parts(96, 3072)
        + parts(384, 768)
        + (
            jax.ShapeDtypeStruct((96, 3072), bf),
            jax.ShapeDtypeStruct((768, 384), bf),
        ),
        in_specs=[ONCHIP, ONCHIP] + [ANYWHERE] * 16,
        out_specs=(ANYWHERE,) * 8 + (ONCHIP, ONCHIP),
        scratch_shapes=[
            pltpu.VMEM((768, 3072), bf),
            pltpu.VMEM((3072, 768), bf),
            pltpu.VMEM((1152, 3072), bf),
            pltpu.VMEM((1152, 3072), bf),
            pltpu.VMEM((8, 144, 768), bf),
            pltpu.VMEM((8, 144, 768), bf),
            pltpu.VMEM((288, 768), f32),
            pltpu.VMEM((288, 768), f32),
            pltpu.VMEM((768, 3072), bf),
            pltpu.VMEM((3072, 768), bf),
            pltpu.VMEM((768, 1152), bf),
        ]
        + rooms((96, 3072), (96, 1536))
        + rooms((768, 384), (384, 384))
        + [DMA((8,))] * 4
        + [DMA((2,)), DMA((8,)), DMA((8,)), DMA((8,)), DMA((8,)), DMA((8,))],
        compiler_params=pltpu.CompilerParams(
            collective_id=2, has_side_effects=True, vmem_limit_bytes=67043328
        ),
        name="experts",
    )(rows, grads, *up_pieces, *down_pieces, first_grad, second_grad)


def hop(values, bit):
    return lax.ppermute(values, "fsdp", [(f, f ^ bit) for f in range(8)])


def square_next(keep, from_x, from_y):
    f32, bf = jnp.float32, jnp.bfloat16
    return (
        hop((keep[0, 1].astype(f32) + from_x[1].astype(f32)).astype(bf), 4),
        hop((keep[1, 1].astype(f32) + from_y[1].astype(f32)).astype(bf), 2),
    )


class DenseSum:
    def __init__(self, kind, grad, out, own, mate, near, far, line, ssem, rsem, lsem):
        self.kind, self.grad, self.out = kind, grad, out
        self.own, self.mate, self.near, self.far, self.line = own, mate, near, far, line
        self.ssem, self.rsem, self.lsem = ssem, rsem, lsem
        self.d, self.s, self.c = place()
        self.order = (
            flip(flip(self.s, 1), 2),
            flip(self.s, 1),
            flip(self.s, 2),
            self.s,
        )

    def piece(self, f):
        if self.kind == "cols":
            return self.grad.at[pl.ds(pl.multiple_of(96 * f, 96), 96)]
        return self.grad.at[:, pl.ds(pl.multiple_of(384 * f, 384), 384)]

    def half(self, ref, h):
        if self.kind == "cols":
            return ref.at[:, pl.ds(1536 * h, 1536)]
        return ref.at[pl.ds(384 * h, 384)]

    def quarter(self, ref, q):
        if self.kind == "cols":
            return ref.at[:, pl.ds(pl.multiple_of(768 * q, 768), 768)]
        return ref.at[pl.ds(pl.multiple_of(192 * q, 192), 192)]

    def start(self):
        d, s, c = self.d, self.s, self.c
        self.zero, self.local = [], []
        for j, position in enumerate(self.order):
            copy = push(
                self.piece(2 * position + 1 - c), self.mate.at[j], self.ssem.at[j], self.rsem.at[j], at(d, s, 1 - c)
            )
            copy.start()
            self.zero.append(copy)
            copy = pltpu.make_async_copy(self.piece(2 * position + c), self.own.at[j], self.lsem.at[j])
            copy.start()
            self.local.append(copy)

    def merge(self):
        d, s, c = self.d, self.s, self.c
        sx, sy = flip(s, 1), flip(s, 2)
        self.one = []
        for j in range(4):
            self.zero[j].wait_recv()
            self.local[j].wait()
            self.own[j] = (widened(self.own.at[j]) + widened(self.mate.at[j])).astype(jnp.bfloat16)
            if j == 0:
                for h, target in enumerate((sx, sy)):
                    copy = push(
                        self.half(self.own.at[0], h), self.near.at[h], self.ssem.at[4 + h], self.rsem.at[4 + h],
                        at(d, target, c),
                    )
                    copy.start()
                    self.one.append(copy)

    def join(self):
        d, s, c = self.d, self.s, self.c
        sx, sy = flip(s, 1), flip(s, 2)
        for h, j in ((0, 2), (1, 1)):
            self.one[h].wait_recv()
            where = self.half(self.own.at[j], h)
            where[...] = (widened(where) + widened(self.near.at[h])).astype(jnp.bfloat16)
        self.two = []
        for h, target in enumerate((sx, sy)):
            copy = push(
                self.own.at[1 + h], self.far.at[h], self.ssem.at[6 + h], self.rsem.at[6 + h], at(d, target, c)
            )
            copy.start()
            self.two.append(copy)

    def square(self):
        for copy in self.two:
            copy.wait_recv()
        return (
            widened(self.own.at[3]) + widened(self.far.at[0]) + widened(self.far.at[1])
        ).astype(jnp.bfloat16)

    def along(self):
        d, s, c = self.d, self.s, self.c
        self.own[3] = self.square()
        self.three = []
        for k in range(1, 4):
            target = lax.rem(d + k, 4)
            copy = push(
                self.quarter(self.own.at[3], target), self.line.at[k - 1], self.ssem.at[7 + k], self.rsem.at[7 + k],
                at(target, s, c),
            )
            copy.start()
            self.three.append(copy)

    def finish(self):
        total = widened(self.quarter(self.own.at[3], self.d))
        for k in range(1, 4):
            self.three[k - 1].wait_recv()
            total = total + widened(self.line.at[k - 1])
        self.out[...] = total
        self.sent(self.three)

    def close(self):
        self.out[...] = self.square()
        self.sent([])

    def sent(self, more):
        for copy in self.zero + self.one + self.two + more:
            copy.wait_send()


class LineSum:
    def __init__(self, kind, part, out, landing, ssem, rsem):
        self.kind, self.part, self.out, self.landing = kind, part, out, landing
        self.ssem, self.rsem = ssem, rsem
        self.d, self.s, self.c = place()

    def quarter(self, q):
        if self.kind == "cols":
            return self.part.at[:, pl.ds(pl.multiple_of(768 * q, 768), 768)]
        return self.part.at[pl.ds(pl.multiple_of(192 * q, 192), 192)]

    def start(self):
        self.copies = []
        for k in range(1, 4):
            target = lax.rem(self.d + k, 4)
            copy = push(
                self.quarter(target), self.landing.at[k - 1], self.ssem.at[k - 1], self.rsem.at[k - 1],
                at(target, self.s, self.c),
            )
            copy.start()
            self.copies.append(copy)

    def finish(self):
        total = widened(self.quarter(self.d))
        for k in range(3):
            self.copies[k].wait_recv()
            total = total + widened(self.landing.at[k])
        self.out[...] = total
        for copy in self.copies:
            copy.wait_send()


class Ending:
    def __init__(self, keep, from_x, from_y, out, room, stage, landed, last, lsem, ssem, rsem, loaded=None):
        self.out, self.room, self.stage, self.landed, self.last = out, room, stage, landed, last
        self.ssem, self.rsem = ssem, rsem
        self.d, self.s, self.c = place()
        sources = [
            keep.at[0, 0], keep.at[0, 1], keep.at[1, 0], keep.at[1, 1],
            from_x.at[0], from_x.at[1], from_y.at[0], from_y.at[1],
        ]
        self.loads = [
            pltpu.make_async_copy(source, room.at[i], lsem.at[i]) for i, source in enumerate(sources)
        ]
        for i, source in enumerate(loaded or ()):
            self.loads.append(pltpu.make_async_copy(source, landed.at[i], lsem.at[8 + i]))
        self.sent = []

    def load(self):
        for copy in self.loads:
            copy.start()

    def loaded(self):
        for copy in self.loads:
            copy.wait()

    def go(self, index, target):
        dst = self.last if index == 2 else self.landed.at[index]
        copy = push(self.stage.at[index], dst, self.ssem.at[index], self.rsem.at[index], target)
        copy.start()
        self.sent.append(copy)

    def next(self):
        bf = jnp.bfloat16
        room = self.room
        self.stage[0] = (widened(room.at[1]) + widened(room.at[5])).astype(bf)
        self.go(0, at(self.d, flip(self.s, 2), self.c))
        self.stage[1] = (widened(room.at[3]) + widened(room.at[7])).astype(bf)
        self.go(1, at(self.d, flip(self.s, 1), self.c))

    def close(self):
        for copy in self.sent:
            copy.wait_recv()
        c = self.c
        mine, theirs = c, 1 - c

        def total(h):
            return (
                widened(self.room.at[2 * h]) + widened(self.room.at[4 + 2 * h]) + widened(self.landed.at[h])
            )

        self.stage[2] = total(theirs).astype(jnp.bfloat16)
        self.go(2, at(self.d, self.s, 1 - c))
        self.out[c] = total(mine)

    def finish(self):
        self.sent[-1].wait_recv()
        self.out[1 - self.c] = widened(self.last)
        for copy in self.sent:
            copy.wait_send()


class Tail:
    def __init__(self, d_rows, router, act, ada, ada_out, d_act_out, router_out, z1, plane, plane_in, z2, z2_in, sems):
        self.d_rows, self.router, self.act, self.ada = d_rows, router, act, ada
        self.ada_out, self.d_act_out, self.router_out = ada_out, d_act_out, router_out
        self.z1, self.plane, self.plane_in, self.z2, self.z2_in = z1, plane, plane_in, z2, z2_in
        self.sems = sems
        self.d, self.s, self.c = place()
        self.f = 2 * self.s + self.c

    def z_copy(self, k, src, dst, base):
        send, recv = self.sems[base], self.sems[base + 1]
        return push(src, dst, send.at[k], recv.at[k], at(lax.rem(self.d + k, 4), self.s, self.c))

    def f_copy(self, k, src, dst, base):
        send, recv = self.sems[base], self.sems[base + 1]
        return push(src, dst, send.at[k], recv.at[k], (self.d, lax.rem(self.f + k, 8)))

    def start(self):
        self.all = [
            self.z_copy(k, self.d_rows.at[lax.rem(self.d + k, 4)], self.z1.at[k], 0) for k in range(1, 4)
        ]
        for copy in self.all:
            copy.start()

    def second(self):
        total = self.d_rows[self.d]
        for k in range(1, 4):
            self.all[k - 1].wait_recv()
            total = total + self.z1[k]
        for target in range(8):
            self.plane[target, :, 0:1152] = total
            self.plane[target, :, 1152:1280] = self.router[target]
        copies = [
            self.f_copy(k, self.plane.at[lax.rem(self.f + k, 8)], self.plane_in.at[lax.rem(8 - k, 8)], 2)
            for k in range(1, 8)
        ]
        for copy in copies:
            copy.start()
        self.in_plane = copies
        self.all = self.all + copies

    def third(self):
        f = self.f
        self.plane_in[0] = self.plane[f]
        for copy in self.in_plane:
            copy.wait_recv()
        everything = self.plane_in[...]
        router = jnp.sum(everything[:, :, 1152:1280], axis=0)
        rows = everything[:, :, 0:1152].reshape(64, 1152)
        line = lax.broadcasted_iota(jnp.int32, (64, 64), 0)
        column = lax.broadcasted_iota(jnp.int32, (64, 64), 1)
        turn = (lax.rem(line // 8 + 8 - f, 8) * 8 + lax.rem(line, 8) == column).astype(jnp.bfloat16)
        d_mod = nn(turn, rows.astype(jnp.bfloat16)).astype(jnp.bfloat16)
        self.ada_out[...] = tn(self.act[...], d_mod)[0:96]
        part = nt(d_mod, self.ada[...])
        self.z2[0:64, 0:96] = part
        self.z2[0:64, 96:128] = jnp.zeros((64, 32), jnp.float32)
        self.z2[64:72, :] = router
        copies = [self.z_copy(k, self.z2, self.z2_in.at[k], 4) for k in range(1, 4)]
        for copy in copies:
            copy.start()
        self.along = copies
        self.all = self.all + copies

    def fourth(self):
        total = self.z2[...]
        for k in range(1, 4):
            self.along[k - 1].wait_recv()
            total = total + self.z2_in[k]
        self.router_out[...] = total[64:72]
        self.z2_in[0] = total
        copies = [
            self.f_copy(
                k,
                self.z2_in.at[0, pl.ds(pl.multiple_of(8 * lax.rem(self.f + k, 8), 8), 8)],
                self.d_act_out.at[self.f],
                6,
            )
            for k in range(1, 8)
        ]
        for copy in copies:
            copy.start()
        self.d_act_out[self.f] = self.z2_in[0, pl.ds(pl.multiple_of(8 * self.f, 8), 8)]
        self.last = copies
        self.all = self.all + copies

    def finish(self):
        for k in range(1, 8):
            self.f_copy(
                k, self.z2_in.at[0, pl.ds(0, 8)], self.d_act_out.at[lax.rem(self.f + 8 - k, 8)], 6
            ).wait_recv()
        for copy in self.all:
            copy.wait_send()


def dense_kernel(
    grad, first_part, second_part, d_rows, router, act, ada,
    up_keep, up_x, up_y, up_low, up_high, down_keep, down_x, down_y,
    out, first_out, second_out, ada_out, d_act_out, router_out, up_out, down_out,
    ur, us, ul, ue, ula, usa, ura, dr, ds, dl, de, dla, dsa, dra,
    own, mate, near, far, line, ssem, rsem, lsem,
    first_in, fs, fr, second_in, ss, sr, *rest,
):
    d, s, c = place()
    f = 2 * s + c
    greet(
        [at(lax.rem(d + k, 4), s, c) for k in range(1, 4)]
        + [(d, lax.rem(f + k, 8)) for k in range(1, 8)]
    )
    dense = DenseSum("cols", grad, out, own, mate, near, far, line, ssem, rsem, lsem)
    lines = (
        LineSum("cols", first_part, first_out, first_in, fs, fr),
        LineSum("rows", second_part, second_out, second_in, ss, sr),
    )
    tail = Tail(d_rows, router, act, ada, ada_out, d_act_out, router_out, *rest[:5], rest[5:])
    ups = Ending(up_keep, up_x, up_y, up_out, ur, us, ul, ue, ula, usa, ura, (up_low, up_high))
    downs = Ending(down_keep, down_x, down_y, down_out, dr, ds, dl, de, dla, dsa, dra)
    tail.start()
    dense.start()
    for each in lines:
        each.start()
    downs.load()
    ups.load()
    tail.second()
    dense.merge()
    tail.third()
    downs.loaded()
    ups.loaded()
    ups.close()
    dense.join()
    downs.next()
    tail.fourth()
    dense.along()
    downs.close()
    for each in lines:
        each.finish()
    ups.finish()
    dense.finish()
    downs.finish()
    tail.finish()


def dense_sums(grad, first_part, second_part, small, routed):
    bf, f32 = jnp.bfloat16, jnp.float32

    def rooms(r, n):
        return [
            pltpu.VMEM((8, r, n), bf),
            pltpu.VMEM((3, r, n), bf),
            pltpu.VMEM((2, r, n), bf),
            pltpu.VMEM((r, n), bf),
            DMA((10,)),
            DMA((3,)),
            DMA((3,)),
        ]

    return pl.pallas_call(
        dense_kernel,
        out_shape=(
            jax.ShapeDtypeStruct((96, 768), f32),
            jax.ShapeDtypeStruct((96, 768), f32),
            jax.ShapeDtypeStruct((192, 384), f32),
            jax.ShapeDtypeStruct((96, 1152), f32),
            jax.ShapeDtypeStruct((8, 8, 128), f32),
            jax.ShapeDtypeStruct((8, 128), f32),
            jax.ShapeDtypeStruct((2, 96, 3072), f32),
            jax.ShapeDtypeStruct((2, 384, 768), f32),
        ),
        in_specs=[ANYWHERE] + [ONCHIP] * 6 + [ANYWHERE] * 8,
        out_specs=(ONCHIP,) * 8,
        scratch_shapes=rooms(96, 3072) + rooms(384, 768) + [
            pltpu.VMEM((4, 96, 3072), bf),
            pltpu.VMEM((4, 96, 3072), bf),
            pltpu.VMEM((2, 96, 1536), bf),
            pltpu.VMEM((2, 96, 3072), bf),
            pltpu.VMEM((3, 96, 768), bf),
            DMA((11,)), DMA((11,)), DMA((4,)),
            pltpu.VMEM((3, 96, 768), bf),
            DMA((3,)), DMA((3,)),
            pltpu.VMEM((3, 192, 384), bf),
            DMA((3,)), DMA((3,)),
            pltpu.VMEM((4, 8, 1152), f32),
            pltpu.VMEM((8, 8, 1280), f32),
            pltpu.VMEM((8, 8, 1280), f32),
            pltpu.VMEM((72, 128), f32),
            pltpu.VMEM((4, 72, 128), f32),
            DMA((4,)), DMA((4,)), DMA((8,)), DMA((8,)), DMA((4,)), DMA((4,)), DMA((8,)), DMA((8,)),
        ],
        compiler_params=pltpu.CompilerParams(
            collective_id=3, has_side_effects=True, vmem_limit_bytes=60 << 20
        ),
        cost_estimate=pl.CostEstimate(flops=40_000_000_000, bytes_accessed=20_000_000, transcendentals=0),
        name="dense_sums",
    )(grad, first_part, second_part, *small, *routed)


def layer_stats(values_in):
    centred = values_in - jnp.mean(values_in, axis=-1, keepdims=True)
    inv_std = lax.rsqrt(jnp.mean(centred * centred, axis=-1, keepdims=True) + 1e-06)
    return centred * inv_std, inv_std


def modulated(inside, mod, part):
    columns = slice(768 * part, 768 * part + 768)
    return inside[:, 0:1] * mod[0:1, columns] + inside[:, 1:2] * mod[1:2, columns]


def head_column(g):
    return 768 * (g // 9) + 64 * (g % 9)


QUERY_ROWS = 256


def front_kernel(
    tokens, mod, inside, seg_col, seg_row, qkvo, router, cotangent, routes, target,
    heads, totals, attended, projected, residual, second, d_mixed, gates, rows, grads,
    bias, made, weighted,
):
    bf, f32 = jnp.bfloat16, jnp.float32
    token_float = tokens[...].astype(f32)
    normed, _ = layer_stats(token_float)
    first = (normed * (1.0 + modulated(inside, mod, 1)) + modulated(inside, mod, 0)).astype(bf)
    for j in range(4):
        piece = nn(first, qkvo[:, 768 * j : 768 * j + 640]).astype(bf)
        for i in range(9):
            heads[9 * j + i] = piece[:, 64 * i : 64 * i + 64]
    bias[...] = jnp.where(seg_col[...] == seg_row[...], 0.0, -1e30)

    def block(n, carry):
        h, part = n // (512 // QUERY_ROWS), lax.rem(n, 512 // QUERY_ROWS)
        lines = pl.ds(pl.multiple_of(part * QUERY_ROWS, QUERY_ROWS), QUERY_ROWS)
        scores = nt(heads[h, lines], heads[12 + h]) * 0.125 + bias[lines]
        row_max = jnp.max(scores, axis=-1, keepdims=True)
        weight = jnp.exp(scores - row_max)
        running = jnp.sum(weight, axis=-1, keepdims=True)
        probability = (weight * (1.0 / running)).astype(bf)
        made[h, lines] = nn(probability, heads[24 + h]).astype(bf)
        totals[h, lines] = row_max + jnp.log(running)
        return carry

    lax.fori_loop(0, 12 * (512 // QUERY_ROWS), block, 0)
    for h in range(12):
        attended[:, 64 * h : 64 * h + 64] = made[h]
    for j in range(4):
        piece = nn(attended[...], qkvo[:, 768 * j + 512 : 768 * j + 768])
        projected[:, 192 * j : 192 * j + 192] = piece[:, 64:256]
    residual[...] = token_float + modulated(inside, mod, 2) * projected[...]
    normed, _ = layer_stats(residual[...])
    second[...] = (normed * (1.0 + modulated(inside, mod, 4)) + modulated(inside, mod, 3)).astype(bf)
    logits = nn(second[...], router[...])
    ids = lax.broadcasted_iota(jnp.int32, (512, 8), 1)
    chosen = [
        jnp.sum(jnp.where(ids == routes[:, k : k + 1], logits, 0.0), axis=-1, keepdims=True)
        for k in range(2)
    ]
    top = jnp.maximum(chosen[0], chosen[1])
    raised = [jnp.exp(each - top) for each in chosen]
    share = [each / (raised[0] + raised[1]) for each in raised]
    pair = lax.broadcasted_iota(jnp.int32, (512, 2), 1)
    gates[...] = jnp.where(pair == 0, share[0], share[1])
    mixed_grad = modulated(inside, mod, 5) * cotangent[...].astype(f32)
    d_mixed[...] = mixed_grad.astype(bf)
    for k in range(2):
        weighted[k] = (share[k] * mixed_grad).astype(bf)

    def send(b, carry):
        lines = pl.ds(pl.multiple_of(288 * b, 288), 288)
        places = lax.broadcasted_iota(jnp.int32, (288, 512), 0) + 288 * b
        first_hot = (places == target[0:1]).astype(f32)
        second_hot = (places == target[1:2]).astype(f32)
        rows[lines] = nn((first_hot + second_hot).astype(bf), second[...]).astype(bf)
        grads[lines] = (
            nn(first_hot.astype(bf), weighted[0]) + nn(second_hot.astype(bf), weighted[1])
        ).astype(bf)
        return carry

    lax.fori_loop(0, 4, send, 0)


def front(tokens, mod, inside, seg_col, seg_row, qkvo, router, cotangent, routes, target):
    bf, f32 = jnp.bfloat16, jnp.float32
    return pl.pallas_call(
        front_kernel,
        out_shape=(
            jax.ShapeDtypeStruct((36, 512, 64), bf),
            jax.ShapeDtypeStruct((12, 512, 1), f32),
            jax.ShapeDtypeStruct((512, 768), bf),
            jax.ShapeDtypeStruct((512, 768), f32),
            jax.ShapeDtypeStruct((512, 768), f32),
            jax.ShapeDtypeStruct((512, 768), bf),
            jax.ShapeDtypeStruct((512, 768), bf),
            jax.ShapeDtypeStruct((512, 2), f32),
            jax.ShapeDtypeStruct((1152, 768), bf),
            jax.ShapeDtypeStruct((1152, 768), bf),
        ),
        in_specs=[ONCHIP] * 10,
        out_specs=(ONCHIP,) * 10,
        scratch_shapes=[
            pltpu.VMEM((512, 512), f32),
            pltpu.VMEM((12, 512, 64), bf),
            pltpu.VMEM((2, 512, 768), bf),
        ],
        compiler_params=pltpu.CompilerParams(vmem_limit_bytes=60 << 20),
        cost_estimate=pl.CostEstimate(flops=40_000_000_000, bytes_accessed=20_000_000, transcendentals=0),
        name="front",
    )(tokens, mod, inside, seg_col, seg_row, qkvo, router, cotangent, routes, target)


def norm_grad(upstream, normed, inv_std):
    return (
        upstream
        - jnp.mean(upstream, axis=-1, keepdims=True)
        - normed * jnp.mean(upstream * normed, axis=-1, keepdims=True)
    ) * inv_std


def rear_kernel(
    tokens, mod, inside, seg_col, seg_row, qkvo, router, cotangent, routes, target,
    heads, totals, attended, projected, residual, second, gates,
    returned, d_returned, shared_out, d_shared,
    output, tokens_grad, qkvo_grad, d_mod, router_grad,
    bias, rows_t, d_heads, d_att, d_att_t, d_rows_t, d_rows, d_residual, d_proj,
):
    bf, f32 = jnp.bfloat16, jnp.float32
    upstream = cotangent[...].astype(f32)

    def image_sums(part, values):
        for j in range(2):
            d_mod[j : j + 1, 768 * part : 768 * part + 768] = jnp.sum(
                inside[:, j : j + 1] * values, axis=0, keepdims=True
            )

    share = [gates[:, k : k + 1] for k in range(2)]
    places = lax.broadcasted_iota(jnp.int32, (512, 1152), 1)
    hot = [(places == target[:, k : k + 1]).astype(f32).astype(bf) for k in range(2)]
    picked = [nn(each, returned[...]) for each in hot]
    mixed = shared_out[...] + (share[0] * picked[0] + share[1] * picked[1])
    gate_two = modulated(inside, mod, 5)
    output[...] = (residual[...] + gate_two * mixed).astype(bf)
    image_sums(5, upstream * mixed)
    mixed_grad = gate_two * upstream
    d_share = [jnp.sum(mixed_grad * each, axis=-1, keepdims=True) for each in picked]
    inner = share[0] * d_share[0] + share[1] * d_share[1]
    ids = lax.broadcasted_iota(jnp.int32, (512, 8), 1)
    d_logits = sum(
        jnp.where(ids == routes[:, k : k + 1], share[k] * (d_share[k] - inner), 0.0) for k in range(2)
    ).astype(bf)
    router_grad[...] = tn(d_logits, second[...])
    d_second = (
        d_shared[...] + nt(d_logits, router[...]) + (nn(hot[0], d_returned[...]) + nn(hot[1], d_returned[...]))
    )
    normed, inv_std = layer_stats(residual[...])
    image_sums(3, d_second)
    image_sums(4, d_second * normed)
    d_residual[...] = upstream + norm_grad(d_second * (1.0 + modulated(inside, mod, 4)), normed, inv_std)
    gate_one = modulated(inside, mod, 2)
    image_sums(2, d_residual[...] * projected[...])
    d_proj[...] = (gate_one * d_residual[...]).astype(bf)
    d_attended = jnp.zeros((512, 768), f32)
    for j in range(4):
        piece = jnp.concatenate(
            [jnp.zeros((512, 64), bf), d_proj[:, 192 * j : 192 * j + 192]], axis=1
        )
        d_attended += nt(piece, qkvo[:, 768 * j + 512 : 768 * j + 768])
    d_attended = d_attended.astype(bf)
    d_att_t[...] = d_attended.T
    for h in range(12):
        d_att[h] = d_attended[:, 64 * h : 64 * h + 64]
    for j in range(18):
        pair = jnp.concatenate([heads[2 * j], heads[2 * j + 1]], axis=1)
        rows_t[128 * j : 128 * j + 128] = pair.T
    bias[...] = jnp.where(seg_col[...] == seg_row[...], 0.0, -1e30)

    def head(h, carry):
        def at_head(g):
            return pl.ds(pl.multiple_of(64 * g, 64), 64)

        d_key, d_value = jnp.zeros((64, 512), f32), jnp.zeros((64, 512), f32)
        for part in range(512 // QUERY_ROWS):
            lines = slice(part * QUERY_ROWS, (part + 1) * QUERY_ROWS)
            scores = nn(heads[h, lines], rows_t[at_head(12 + h)]) * 0.125 + bias[lines]
            probability = jnp.exp(scores - totals[h, lines])
            d_prob = nn(d_att[h, lines], rows_t[at_head(24 + h)])
            inner = jnp.sum(probability * d_prob, axis=-1, keepdims=True)
            d_scores = (probability * (d_prob - inner)).astype(bf)
            d_heads[h, lines] = (nn(d_scores, heads[12 + h]) * 0.125).astype(bf)
            d_key += nn(rows_t[at_head(h), lines], d_scores)
            d_value += nn(d_att_t[at_head(h), lines], probability.astype(bf))
        d_rows_t[at_head(h)] = (d_key * 0.125).astype(bf)
        d_rows_t[at_head(12 + h)] = d_value.astype(bf)
        return carry

    lax.fori_loop(0, 12, head, 0)
    for g in range(12):
        column = head_column(g)
        d_rows[:, column : column + 64] = d_heads[g]
    for j in range(12):
        pair = d_rows_t[128 * j : 128 * j + 128].T
        for i in range(2):
            column = head_column(12 + 2 * j + i)
            d_rows[:, column : column + 64] = pair[:, 64 * i : 64 * i + 64]
    for j in range(4):
        d_rows[:, 768 * j + 576 : 768 * j + 768] = jnp.zeros((512, 192), bf)
    token_float = tokens[...].astype(f32)
    normed, inv_std = layer_stats(token_float)
    scale_one = 1.0 + modulated(inside, mod, 1)
    first_t = (normed * scale_one + modulated(inside, mod, 0)).astype(bf).T
    attended_t = attended[...].T
    for j in range(4):
        qkvo_grad[:, 768 * j : 768 * j + 640] = nn(first_t, d_rows[:, 768 * j : 768 * j + 640]).astype(bf)
        qkvo_grad[:, 768 * j + 576 : 768 * j + 768] = nn(
            attended_t, d_proj[:, 192 * j : 192 * j + 192]
        ).astype(bf)
    d_first = nt(d_rows[...], qkvo[...])
    image_sums(0, d_first)
    image_sums(1, d_first * normed)
    tokens_grad[...] = d_residual[...] + norm_grad(d_first * scale_one, normed, inv_std)


def rear(*operands):
    bf, f32 = jnp.bfloat16, jnp.float32
    return pl.pallas_call(
        rear_kernel,
        out_shape=(
            jax.ShapeDtypeStruct((512, 768), bf),
            jax.ShapeDtypeStruct((512, 768), f32),
            jax.ShapeDtypeStruct((768, 3072), bf),
            jax.ShapeDtypeStruct((2, 4608), f32),
            jax.ShapeDtypeStruct((8, 768), f32),
        ),
        in_specs=[ONCHIP] * len(operands),
        out_specs=(ONCHIP,) * 5,
        scratch_shapes=[
            pltpu.VMEM((512, 512), f32),
            pltpu.VMEM((2304, 512), bf),
            pltpu.VMEM((12, 512, 64), bf),
            pltpu.VMEM((12, 512, 64), bf),
            pltpu.VMEM((768, 512), bf),
            pltpu.VMEM((1536, 512), bf),
            pltpu.VMEM((512, 3072), bf),
            pltpu.VMEM((512, 768), f32),
            pltpu.VMEM((512, 768), bf),
        ],
        compiler_params=pltpu.CompilerParams(vmem_limit_bytes=67043328),
        cost_estimate=pl.CostEstimate(flops=60_000_000_000, bytes_accessed=30_000_000, transcendentals=0),
        name="rear",
    )(*operands)


def fitted_shards(
    tokens,
    condition,
    ada_weight,
    qkv_weight,
    out_weight,
    shared_up,
    shared_down,
    router_weight,
    expert_up,
    expert_down,
    routes,
    image_sizes,
    cotangent,
):
    bf = jnp.bfloat16
    d_index, f_index = lax.axis_index("dp"), lax.axis_index("fsdp")
    model_width = tokens.shape[1]
    head_size = model_width // HEADS
    inside, segment = owners(image_sizes)
    ids = jnp.arange(EXPERTS, dtype=jnp.int32)
    hot = routes[:, :, None] == ids[None, None, :]
    hot_any = jnp.any(hot, axis=1).astype(bf)
    order = jnp.arange(LONG, dtype=jnp.int32)
    earlier = (order[:, None] > order[None, :]).astype(bf)
    before = nn(earlier, hot_any)
    position = jnp.sum(jnp.where(hot, before[:, None, :], 0.0), axis=-1).astype(jnp.int32)
    target = routes * CAP + position
    live = (segment < IMG_DEV).astype(jnp.float32)
    counts = jnp.sum(live[:, None] * hot_any.astype(jnp.float32), axis=0)
    cond_float = condition.astype(jnp.float32)
    activated = jax.nn.silu(cond_float).astype(bf)
    act_slices = activated.astype(jnp.float32).reshape(IMG_DEV, 8, 96).transpose(1, 0, 2)
    act_slices = jnp.pad(act_slices, ((0, 0), (0, 6), (0, 32)))
    act_slices = act_slices.at[:, 2, :EXPERTS].set(counts)
    ada_pad = jnp.pad(ada_weight, ((0, 32), (0, 0)))
    router_pack = jnp.pad(router_weight.reshape(192), (0, 2048 - 192)).reshape(16, 128)
    qkvo_shard = jnp.concatenate([qkv_weight, out_weight], axis=1)
    qkvo, routers, seen, mod_rows, up_line, down_line, up_m, up_x0, up_y0, down_own, down_m = opening(
        qkvo_shard, router_pack, act_slices, ada_pad, shared_up, shared_down.T, expert_up, expert_down
    )
    hops = hop(up_m, 2), hop(up_m, 4), hop(down_own, 2), hop(down_own, 4)
    expert_counts = seen[66, :EXPERTS].astype(jnp.int32)
    modulation = lax.dynamic_slice(mod_rows, (0, 2 * d_index, 0), (4, 2, 1152))
    modulation = modulation.transpose(1, 0, 2).reshape(2, 4608)
    router_full = (
        routers.reshape(32, 2048)[:, :192]
        .reshape(4, 8, 96, 2)
        .transpose(1, 2, 0, 3)
        .reshape(model_width, EXPERTS)
    )
    segments = (segment[:, None], segment[None, :])
    heads, totals, attended, projected, residual, second_input, d_mixed, gates, rows, grads = front(
        tokens, modulation, inside, *segments, qkvo, router_full, cotangent, routes, target.T
    )
    rows = rows.reshape(EXPERTS, CAP, model_width)
    grads = grads.reshape(EXPERTS, CAP, model_width)
    rows, (up_x1, up_y1, down_x0, down_y0) = lax.optimization_barrier((rows, hops))
    rows_in, grads_in, up_corner, down_x1, down_y1, down_corner, shared_out, d_second, *shared_grads = (
        outbound(
            rows, grads, up_line, down_line, second_input, d_mixed, up_x0, up_y1, down_m, down_x0
        )
    )
    returned, d_returned, up_keep, *up_near, down_keep, down_x, down_y, first_part, second_part = experts(
        rows_in, grads_in, (expert_up, up_m, up_x0, up_x1, up_y0, up_y1, up_corner),
        (down_own, down_m, down_x0, down_x1, down_y0, down_y1, down_corner),
        *shared_grads,
    )
    up_next = square_next(up_keep, *up_near)
    down_near = hop(down_x, 2), hop(down_y, 4)
    returned = returned.reshape(EXPERTS * CAP, model_width)
    d_returned = d_returned.reshape(EXPERTS * CAP, model_width)
    output, tokens_grad, qkvo_grad, d_modulation, router_grad = rear(
        tokens, modulation, inside, *segments, qkvo, router_full, cotangent, routes, target,
        heads, totals, attended, projected, residual, second_input, gates,
        returned, d_returned, shared_out, d_second,
    )
    qkvo_grad, down_near, up_next = lax.optimization_barrier((qkvo_grad, down_near, up_next))
    d_modulation = d_modulation.astype(bf)
    d_mod_rows = d_modulation.astype(jnp.float32).reshape(2, 4, 1152).transpose(1, 0, 2)
    d_mod_rows = lax.dynamic_update_slice(
        jnp.zeros((4, 8, 1152), jnp.float32), d_mod_rows, (0, 2 * d_index, 0)
    )
    router_tiles = jnp.pad(
        router_grad.reshape(EXPERTS, 8, 96).transpose(1, 0, 2), ((0, 0), (0, 0), (0, 32))
    )
    (
        qkvo_sum, shared_first_sum, shared_second_sum, ada_grad, d_act_tiles, router_sum,
        expert_up_grad, expert_down_grad,
    ) = dense_sums(
        qkvo_grad, first_part, second_part,
        (d_mod_rows, router_tiles, seen[:64].astype(bf), ada_weight),
        (up_keep, *up_near, *up_next, down_keep, *down_near),
    )
    d_activated = lax.dynamic_slice(d_act_tiles, (0, 2 * d_index, 0), (8, 2, 96))
    d_activated = d_activated.transpose(1, 0, 2).reshape(2, model_width)
    condition_grad = jax.vjp(jax.nn.silu, cond_float)[1](d_activated)[0]
    router_out = lax.dynamic_slice(router_sum, (2 * d_index, 0), (2, 96)).T
    return (
        output,
        tokens_grad,
        condition_grad,
        ada_grad,
        qkvo_sum[:, :576],
        qkvo_sum[:, 576:],
        shared_first_sum,
        shared_second_sum.T,
        router_out,
        expert_up_grad,
        expert_down_grad,
        expert_counts,
    )


def solution(mesh):
    placed = (
        P(("dp", "fsdp"), None),
        P(("dp", "fsdp"), None),
        P("fsdp", "dp"),
        P("fsdp", "dp"),
        P("fsdp", "dp"),
        P("fsdp", "dp"),
        P("fsdp", "dp"),
        P("fsdp", "dp"),
        P("dp", "fsdp", None),
        P("dp", "fsdp", None),
        P(("dp", "fsdp"), None),
        P(("dp", "fsdp")),
        P(("dp", "fsdp"), None),
    )
    fitted = mesh.shape["dp"] == 4 and mesh.shape["fsdp"] == 8
    return jax.shard_map(
        fitted_shards if fitted else shards,
        mesh=mesh,
        in_specs=placed,
        out_specs=(
            P(("dp", "fsdp"), None),
            P(("dp", "fsdp"), None),
            P(("dp", "fsdp"), None),
            P("fsdp", "dp"),
            P("fsdp", "dp"),
            P("fsdp", "dp"),
            P("fsdp", "dp"),
            P("fsdp", "dp"),
            P("fsdp", "dp"),
            P("dp", "fsdp", None),
            P("dp", "fsdp", None),
            P(),
        ),
        check_vma=False,
    )
```

profile of v0, /device:TPU:0, one launch (start us, length us, event | category | flops | bytes accessed | tf_op | source)
XLA Modules:
  0.0 429.5 jit_solution(933693871466030026)
XLA Ops:
  6.2 1.7 pad.26.ada_ref
  7.9 1.7 pad_maximum_fusion.shard
  10.4 59.0 %opening.1 = (bf16[768,3072]{1,0:T(8,128)(2,1)}, bf16[32,16,128]{2,1,0:T(8,128)(2,1)}, f32[72,128]{1,0:T(8,128)}, f32[4,8,1152]{2,1,0:T(8,128)}, bf16[96,3072]{1...) custom-call(bf16[96,768]{1,0:T(8,128)(2,1)} %pad_maximum_fusion.shar, ...), custom_call_target="tpu_custom_call" | custom-call | tf_op jit(solution)/shard_map/opening/pallas_call | solution.py:823
  69.4 1.4 collective-permute-start
  70.8 1.4 collective-permute-start.1
  74.6 1.2 copy.78
  78.6 1.5 constant_dynamic-slice_fusion
  80.1 32.3 %front.1 = (bf16[36,512,64]{2,1,0:T(8,128)(2,1)}, f32[12,512,1]{2,1,0:T(8,128)}, bf16[512,768]{1,0:T(8,128)(2,1)}, f32[512,768]{1,0:T(8,128)}, f32[512,768]{1,0:...) custom-call(bf16[512,768]{1,0:T(8,128)(2,1)} %tokens.3, ...), custom_call_target="tpu_custom_call" | custom-call | flops 40000000000 | bytes 20000000 | tf_op jit(solution)/shard_map/front/pallas_call | solution.py:1720
  113.2 1.4 slice.71.act
  116.8 88.9 %outbound.1 = (bf16[8,144,768]{2,1,0:T(8,128)(2,1)}, bf16[8,144,768]{2,1,0:T(8,128)(2,1)}, bf16[2,96,3072]{2,1,0:T(8,128)(2,1)}, bf16[384,768]{1,0:T(8,128)(2,1)...) custom-call(bf16[8,144,768]{2,1,0:T(8,128)(2,1)} %bitcast.56, ...), custom_call_target="tpu_custom_call" | custom-call | tf_op jit(solution)/shard_map/outbound/pallas_call | solution.py:988
  205.8 102.0 %experts.1 = (bf16[8,144,768]{2,1,0:T(8,128)(2,1)}, bf16[8,144,768]{2,1,0:T(8,128)(2,1)}, bf16[2,2,96,3072]{3,2,1,0:T(8,128)(2,1)}, bf16[2,96,3072]{2,1,0:T(8,12...) custom-call(bf16[8,144,768]{2,1,0:T(8,128)(2,1)} %get-tuple-element., ...), custom_call_target="tpu_custom_call" | custom-call | tf_op jit(solution)/shard_map/experts/pallas_call | solution.py:1186
  307.7 3.0 fusion
  310.8 1.3 collective-permute-start.6
  312.0 1.5 collective-permute-start.7
  314.8 43.5 %rear.1 = (bf16[512,768]{1,0:T(8,128)(2,1)}, f32[512,768]{1,0:T(8,128)}, bf16[768,3072]{1,0:T(8,128)(2,1)}, f32[2,4608]{1,0:T(2,128)}, f32[8,768]{1,0:T(8,128)}) custom-call(bf16[512,768]{1,0:T(8,128)(2,1)} %tokens.3, f32[2,4608]{1,0:T(2,128)} %bitcast.65, f32[512,2]{1,0:T(8,128)} %get-tuple-element.156.inside, s32[512,1]{1,0:T(8,128)} %copy.72.seg_col, ...), custom_call_target="tpu_custom_call" | custom-call | flops 60000002048 | bytes 30000000 | tf_op jit(solution)/shard_map/rear/pallas_call | solution.py:1860
  361.2 52.8 %dense_sums.1 = (f32[96,768]{1,0:T(8,128)}, f32[96,768]{1,0:T(8,128)}, f32[192,384]{1,0:T(8,128)}, f32[96,1152]{1,0:T(8,128)}, f32[8,8,128]{2,1,0:T(8,128)}, /*i...) custom-call(bf16[768,3072]{1,0:T(8,128)(2,1)} %get-tuple-element.133.grad, ...), custom_call_target="tpu_custom_call" | custom-call | flops 40000000000 | bytes 20000000 | tf_op jit(solution)/shard_map/dense_sums/pallas_call | solution.py:1594
  414.0 1.8 slice.60
  415.8 1.6 slice.61
  418.9 1.3 dynamic-slice_bitcast_fusion.1
  420.2 1.8 copy.90
  422.0 1.7 copy.91
  423.7 1.7 copy.92
  425.4 1.4 copy.93
  427.9 1.4 copy.94
  (74 shorter events, 21.3 us)
Async XLA Ops:
  6.1 71.0 %copy-start.11 = (s32[512]{0:T(512)}, s32[512]{0:T(512)S(1)}, u32[]{:S(2)}) copy-start(s32[512]{0:T(512)S(1)} %get-tuple-element.153) | copy-start | bytes 6148
  9.8 0.6 copy-start.7
  10.4 63.3 %copy-start.8 = (s32[512,2]{0,1:T(2,128)S(1)}, s32[512,2]{0,1:T(2,128)}, u32[]{:S(2)}) copy-start(s32[512,2]{0,1:T(2,128)} %param.25) | copy-start | bytes 12292
  69.4 46.4 %collective-permute-start = (bf16[96,3072]{1,0:T(8,128)(2,1)}, bf16[96,3072]{1,0:T(8,128)(2,1)S(1)}, u32[]{:S(2)}, u32[]{:S(2)}) collective-permute-start(bf16[96,3072]{1,0:T(8,128)(2,1)} %get-tuple-element.99.up_m), channel_id=1, source_target_pairs={{0,2},{1,3},{2,0},{3,1},{4,6},{5,7},{6,4},{7,5},{8,10},{9,11},{10,... | collective-permute-start | bytes 1769480 | tf_op jit(solution)/shard_map/ppermute | solution.py:1225
  70.8 45.0 %collective-permute-start.1 = (bf16[96,3072]{1,0:T(8,128)(2,1)}, bf16[96,3072]{1,0:T(8,128)(2,1)S(1)}, u32[]{:S(2)}, u32[]{:S(2)}) collective-permute-start(bf16[96,3072]{1,0:T(8,128)(2,1)} %get-tuple-element.99.up_m), channel_id=1, source_target_pairs={{0,4},{1,5},{2,6},{3,7},{4,0},{5,1},{6,2},{7,3},{8,12},{9,13},{10,... | collective-permute-start | bytes 1769480 | tf_op jit(solution)/shard_map/ppermute | solution.py:1225
  72.2 43.6 %collective-permute-start.2 = (bf16[384,768]{1,0:T(8,128)(2,1)}, bf16[384,768]{1,0:T(8,128)(2,1)S(1)}, u32[]{:S(2)}, u32[]{:S(2)}) collective-permute-start(bf16[384,768]{1,0:T(8,128)(2,1)} %get-tuple-element.100.down_own), channel_id=1, source_target_pairs={{0,2},{1,3},{2,0},{3,1},{4,6},{5,7},{6,4},{7,5},{8,10},{9,11},{10,... | collective-permute-start | bytes 1769480 | tf_op jit(solution)/shard_map/ppermute | solution.py:1225
  72.7 43.1 %collective-permute-start.3 = (bf16[384,768]{1,0:T(8,128)(2,1)}, bf16[384,768]{1,0:T(8,128)(2,1)S(1)}, u32[]{:S(2)}, u32[]{:S(2)}) collective-permute-start(bf16[384,768]{1,0:T(8,128)(2,1)} %get-tuple-element.100.down_own), channel_id=1, source_target_pairs={{0,4},{1,5},{2,6},{3,7},{4,0},{5,1},{6,2},{7,3},{8,12},{9,13},{10,... | collective-permute-start | bytes 1769480 | tf_op jit(solution)/shard_map/ppermute | solution.py:1225
  80.1 32.3 %copy-start.9 = (s32[512,2]{0,1:T(2,128)S(1)}, s32[512,2]{0,1:T(2,128)}, u32[]{:S(2)}) copy-start(s32[512,2]{0,1:T(2,128)} %convert_add_fusion.2) | copy-start | bytes 12292
  115.8 89.9 %copy-start.4 = (bf16[96,3072]{1,0:T(8,128)(2,1)}, bf16[96,3072]{1,0:T(8,128)(2,1)S(1)}, u32[]{:S(2)}) copy-start(bf16[96,3072]{1,0:T(8,128)(2,1)S(1)} %collective-permute-done.up_x1) | copy-start | bytes 1769476
  115.8 0.8 copy-start
  115.8 1.0 copy-start.1
  115.8 89.9 %copy-start.5 = (bf16[384,768]{1,0:T(8,128)(2,1)}, bf16[384,768]{1,0:T(8,128)(2,1)S(1)}, u32[]{:S(2)}) copy-start(bf16[384,768]{1,0:T(8,128)(2,1)S(1)} %collective-permute-done.3.down_y0) | copy-start | bytes 1769476
  310.8 49.8 %collective-permute-start.6 = (bf16[96,3072]{1,0:T(8,128)(2,1)}, bf16[96,3072]{1,0:T(8,128)(2,1)}, u32[]{:S(2)}, u32[]{:S(2)}) collective-permute-start(bf16[96,3072]{1,0:T(8,128)(2,1)} %get-tuple-element.155), channel_id=1, source_target_pairs={{0,4},{1,5},{2,6},{3,7},{4,0},{5,1},{6,2},{7,3},{8,12},{9,13},{10,... | collective-permute-start | bytes 1769480 | tf_op jit(solution)/shard_map/ppermute | solution.py:1225
  312.0 48.6 %collective-permute-start.7 = (bf16[96,3072]{1,0:T(8,128)(2,1)}, bf16[96,3072]{1,0:T(8,128)(2,1)}, u32[]{:S(2)}, u32[]{:S(2)}) collective-permute-start(bf16[96,3072]{1,0:T(8,128)(2,1)} %get-tuple-element.154), channel_id=1, source_target_pairs={{0,2},{1,3},{2,0},{3,1},{4,6},{5,7},{6,4},{7,5},{8,10},{9,11},{10,... | collective-permute-start | bytes 1769480 | tf_op jit(solution)/shard_map/ppermute | solution.py:1225
  313.5 47.1 %collective-permute-start.4 = (bf16[2,384,768]{2,1,0:T(8,128)(2,1)}, bf16[2,384,768]{2,1,0:T(8,128)(2,1)}, u32[]{:S(2)}, u32[]{:S(2)}) collective-permute-start(bf16[2,384,768]{2,1,0:T(8,128)(2,1)} %get-tuple-element.128), channel_id=1, source_target_pairs={{0,2},{1,3},{2,0},{3,1},{4,6},{5,7},{6,4},{7,5},{8,10},{9,11},{10,... | collective-permute-start | bytes 3538952 | tf_op jit(solution)/shard_map/ppermute | solution.py:1225
  314.0 46.6 %collective-permute-start.5 = (bf16[2,384,768]{2,1,0:T(8,128)(2,1)}, bf16[2,384,768]{2,1,0:T(8,128)(2,1)}, u32[]{:S(2)}, u32[]{:S(2)}) collective-permute-start(bf16[2,384,768]{2,1,0:T(8,128)(2,1)} %get-tuple-element.129), channel_id=1, source_target_pairs={{0,4},{1,5},{2,6},{3,7},{4,0},{5,1},{6,2},{7,3},{8,12},{9,13},{10,... | collective-permute-start | bytes 3538952 | tf_op jit(solution)/shard_map/ppermute | solution.py:1225
  360.6 0.7 copy-start.6
  361.2 57.1 %copy-start.10 = (bf16[2,768]{1,0:T(2,128)(2,1)S(1)}, bf16[2,768]{1,0:T(2,128)(2,1)}, u32[]{:S(2)}) copy-start(bf16[2,768]{1,0:T(2,128)(2,1)} %param.16) | copy-start | bytes 9220
  414.0 11.4 %copy-start.3 = (f32[2,96,3072]{2,1,0:T(8,128)S(1)}, f32[2,96,3072]{2,1,0:T(8,128)}, u32[]{:S(2)}) copy-start(f32[2,96,3072]{2,1,0:T(8,128)} %get-tuple-element.179) | copy-start | bytes 7077892
  425.4 2.5 copy-start.2
where the time goes:
time: 436 us; the launch traced here: 429 us
  Pallas kernels  378 us (87%)
  local copies, waits for them, and re-layouts  29.8 us (7%)
  other arithmetic  11.9 us (3%)
  starting transfers between devices  8.17 us (2%)
    pallas_call x1, Pallas kernels, experts(): pl.pallas_call(expert_kernel, out_shape=(jax.ShapeDtypeStruct((8, 144, 76...  102 us
    pallas_call x1, Pallas kernels, outbound(): pl.pallas_call(out_kernel, out_shape=(jax.ShapeDtypeStruct((8, 144, 768),...  88.9 us
    pallas_call x1, Pallas kernels, opening(): pl.pallas_call(open_kernel, out_shape=(jax.ShapeDtypeStruct((768, 3072),...  59 us
    pallas_call x1, Pallas kernels, dense_sums(): pl.pallas_call(dense_kernel, out_shape=(jax.ShapeDtypeStruct((96, 768), f...  52.8 us
    pallas_call x1, Pallas kernels, rear(): pl.pallas_call(rear_kernel, out_shape=(jax.ShapeDtypeStruct((512, 768), b...  43.5 us
    pallas_call x1, Pallas kernels, front(): pl.pallas_call(front_kernel, out_shape=(jax.ShapeDtypeStruct((36, 512, 64...  32.3 us
    unnamed x31, local copies, waits for them, and re-layouts  13 us
  transfers between devices with their start and end apart: 8, of which 0 were waited for; matrix products, arithmetic and copies ran while one was open for 3% of the time, Pallas kernels for 18%

commit v1 on v0

--- a/solution.py
+++ b/solution.py
@@ -684,14 +684,16 @@
 
 
 def open_kernel(
-    shard, router, act_ref, ada_ref, up_shard, down_shard, expert_up, expert_down,
-    full, routers, seen, rows_out, up_line, down_line, up_mate, up_x, up_y, down_own, down_mate,
-    heard, part, got, mixed, ssem, rsem, lsem, asem, brsem, rssem, rrsem, tssem, trsem, zssem, zrsem,
+    qkv_shard, out_shard, act_ref, ada_ref, up_shard, down_shard, expert_up, expert_down,
+    full, router_t, seen, rows_out, up_line, down_line, up_mate, up_x, up_y, down_own, down_mate,
+    shard, heard, part, got, mixed, ssem, rsem, lsem, asem, brsem, tssem, trsem, zssem, zrsem,
     us, ur, ds, dr, es, er, el,
 ):
     me, other = everyone_else()
     d, s, c = place()
     f = 2 * s + c
+    shard[:, 0:576] = qkv_shard[...]
+    shard[:, 576:768] = out_shard[...]
     barrier = pltpu.get_barrier_semaphore()
 
     def hello(k, carry):
@@ -704,9 +706,6 @@
     def act_copy(k, source):
         device = other(k)
         return push(act_ref.at[device[1]], heard.at[source], asem.at[k], brsem.at[k], device)
-
-    def router_copy(k, source):
-        return push(router, routers.at[source], rssem.at[k], rrsem.at[k], other(k))
 
     def send(k, carry):
         act_copy(k, me).start()
@@ -718,19 +717,12 @@
     near = Near(
         expert_up, expert_down, up_mate, up_x, up_y, down_own, down_mate, es, er, el.at[0]
     )
-    near.start()
     lines = (
         Line("cols", up_shard, up_line, us, ur, lsem.at[3]),
         Line("rows", down_shard, down_line, ds, dr, lsem.at[4]),
     )
-    own_router = pltpu.make_async_copy(router, routers.at[me], lsem.at[1])
-    own_router.start()
-
-    def send_router(k, carry):
-        router_copy(k, me).start()
-        return carry
-
-    lax.fori_loop(1, 32, send_router, 0)
+    gather.spread_z(1)
+    gather.spread_z(2)
     heard[me] = act_ref[f]
 
     def take(k, carry):
@@ -750,9 +742,10 @@
     seen[...] = jnp.concatenate(
         [compact.astype(jnp.float32), jnp.sum(heard[...], axis=0)], axis=0
     )
-    part[...] = jnp.dot(compact, ada_ref[...], preferred_element_type=jnp.float32).reshape(
-        8, 8, 1152
-    )
+    for column_block in range(8):
+        tiles = [heard[8 * j + column_block, 3:5, 0:96] for j in range(4)]
+        router_t[:, 96 * column_block : 96 * column_block + 96] = jnp.concatenate(tiles, axis=0)
+    part[...] = nn(compact[:, 0:96], ada_ref[...]).reshape(8, 8, 1152)
 
     def tile_copy(k):
         target = lax.rem(f + k, 8)
@@ -760,9 +753,11 @@
 
     for k in range(1, 8):
         tile_copy(k).start()
-    gather.spread_z(1)
-    gather.spread_z(2)
     gather.relay(0)
+    gather.spread_z(3)
+    near.start()
+    gather.relay(1)
+    gather.relay(2)
     for k in range(1, 8):
         tile_copy(k).wait_recv()
     total = part[f]
@@ -776,14 +771,11 @@
         zs.append(copy)
     own_rows = pltpu.make_async_copy(mixed, rows_out.at[d], lsem.at[2])
     own_rows.start()
-    gather.spread_z(3)
     for line in lines:
         line.start()
-    gather.relay(1)
+    gather.relay(3)
     gather.corner(0)
-    gather.relay(2)
     gather.corner(1)
-    gather.relay(3)
     gather.corner(2)
     for line in lines:
         line.relay()
@@ -792,7 +784,6 @@
     for line in lines:
         line.finish()
     near.finish()
-    own_router.wait()
     own_rows.wait()
     for k in range(1, 4):
         push(
@@ -806,9 +797,6 @@
 
     def drain(k, carry):
         act_copy(k, me).wait_send()
-        copy = router_copy(k, lax.rem(me + 32 - k, 32))
-        copy.wait_recv()
-        copy.wait_send()
         return carry
 
     lax.fori_loop(1, 32, drain, 0)
@@ -819,12 +807,12 @@
 ONCHIP = pl.BlockSpec(memory_space=pltpu.VMEM)
 
 
-def opening(shard, router, act, ada, up_shard, down_shard, expert_up, expert_down):
+def opening(*operands):
     return pl.pallas_call(
         open_kernel,
         out_shape=(
             jax.ShapeDtypeStruct((768, 3072), jnp.bfloat16),
-            jax.ShapeDtypeStruct((32, 16, 128), jnp.bfloat16),
+            jax.ShapeDtypeStruct((8, 768), jnp.float32),
             jax.ShapeDtypeStruct((72, 128), jnp.float32),
             jax.ShapeDtypeStruct((4, 8, 1152), jnp.float32),
             jax.ShapeDtypeStruct((96, 3072), jnp.bfloat16),
@@ -833,21 +821,22 @@
         + (jax.ShapeDtypeStruct((96, 3072), jnp.bfloat16),) * 3
         + (jax.ShapeDtypeStruct((384, 768), jnp.bfloat16),) * 2,
         in_specs=[ONCHIP] * 6 + [ANYWHERE] * 2,
-        out_specs=(ANYWHERE, ANYWHERE, ONCHIP) + (ANYWHERE,) * 8,
+        out_specs=(ANYWHERE, ONCHIP, ONCHIP) + (ANYWHERE,) * 8,
         scratch_shapes=[
+            pltpu.VMEM((96, 768), jnp.bfloat16),
             pltpu.VMEM((32, 8, 128), jnp.float32),
             pltpu.VMEM((8, 8, 1152), jnp.float32),
             pltpu.VMEM((8, 8, 1152), jnp.float32),
             pltpu.VMEM((8, 1152), jnp.float32),
             DMA((GATHER_SEMS,)), DMA((GATHER_SEMS,)), DMA((5,)),
-            DMA((32,)), DMA((32,)), DMA((32,)), DMA((32,)),
+            DMA((32,)), DMA((32,)),
             DMA((8,)), DMA((8,)), DMA((4,)), DMA((4,)),
             DMA((3,)), DMA((3,)), DMA((3,)), DMA((3,)),
             DMA((4,)), DMA((4,)), DMA((1,)),
         ],
         compiler_params=pltpu.CompilerParams(collective_id=0, has_side_effects=True),
         name="opening",
-    )(shard, router, act, ada, up_shard, down_shard, expert_up, expert_down)
+    )(*operands)
 
 
 def group_of(d, s, c):
@@ -1637,6 +1626,14 @@
     return centred * inv_std, inv_std
 
 
+def lines_of(tile, first):
+    row = lax.broadcasted_iota(jnp.int32, tile.shape, 0)
+    picked = [
+        jnp.sum(jnp.where(row == first + i, tile, 0.0), axis=0, keepdims=True) for i in range(2)
+    ]
+    return jnp.concatenate(picked, axis=0)
+
+
 def modulated(inside, mod, part):
     columns = slice(768 * part, 768 * part + 768)
     return inside[:, 0:1] * mod[0:1, columns] + inside[:, 1:2] * mod[1:2, columns]
@@ -1650,11 +1647,14 @@
 
 
 def front_kernel(
-    tokens, mod, inside, seg_col, seg_row, qkvo, router, cotangent, routes, target,
-    heads, totals, attended, projected, residual, second, d_mixed, gates, rows, grads,
+    tokens, mod_rows, inside, seg_col, seg_row, qkvo, router_t, cotangent, routes, target,
+    heads, totals, attended, projected, residual, second, d_mixed, gates, rows, grads, mod,
     bias, made, weighted,
 ):
     bf, f32 = jnp.bfloat16, jnp.float32
+    d = lax.axis_index("dp")
+    for j in range(4):
+        mod[:, 1152 * j : 1152 * j + 1152] = lines_of(mod_rows[j], 2 * d)
     token_float = tokens[...].astype(f32)
     normed, _ = layer_stats(token_float)
     first = (normed * (1.0 + modulated(inside, mod, 1)) + modulated(inside, mod, 0)).astype(bf)
@@ -1685,7 +1685,7 @@
     residual[...] = token_float + modulated(inside, mod, 2) * projected[...]
     normed, _ = layer_stats(residual[...])
     second[...] = (normed * (1.0 + modulated(inside, mod, 4)) + modulated(inside, mod, 3)).astype(bf)
-    logits = nn(second[...], router[...])
+    logits = nt(second[...], router_t[...].astype(bf))
     ids = lax.broadcasted_iota(jnp.int32, (512, 8), 1)
     chosen = [
         jnp.sum(jnp.where(ids == routes[:, k : k + 1], logits, 0.0), axis=-1, keepdims=True)
@@ -1715,7 +1715,7 @@
     lax.fori_loop(0, 4, send, 0)
 
 
-def front(tokens, mod, inside, seg_col, seg_row, qkvo, router, cotangent, routes, target):
+def front(*operands):
     bf, f32 = jnp.bfloat16, jnp.float32
     return pl.pallas_call(
         front_kernel,
@@ -1730,9 +1730,10 @@
             jax.ShapeDtypeStruct((512, 2), f32),
             jax.ShapeDtypeStruct((1152, 768), bf),
             jax.ShapeDtypeStruct((1152, 768), bf),
+            jax.ShapeDtypeStruct((2, 4608), f32),
         ),
         in_specs=[ONCHIP] * 10,
-        out_specs=(ONCHIP,) * 10,
+        out_specs=(ONCHIP,) * 11,
         scratch_shapes=[
             pltpu.VMEM((512, 512), f32),
             pltpu.VMEM((12, 512, 64), bf),
@@ -1741,7 +1742,7 @@
         compiler_params=pltpu.CompilerParams(vmem_limit_bytes=60 << 20),
         cost_estimate=pl.CostEstimate(flops=40_000_000_000, bytes_accessed=20_000_000, transcendentals=0),
         name="front",
-    )(tokens, mod, inside, seg_col, seg_row, qkvo, router, cotangent, routes, target)
+    )(*operands)
 
 
 def norm_grad(upstream, normed, inv_std):
@@ -1753,7 +1754,7 @@
 
 
 def rear_kernel(
-    tokens, mod, inside, seg_col, seg_row, qkvo, router, cotangent, routes, target,
+    tokens, mod, inside, seg_col, seg_row, qkvo, router_t, cotangent, routes, target,
     heads, totals, attended, projected, residual, second, gates,
     returned, d_returned, shared_out, d_shared,
     output, tokens_grad, qkvo_grad, d_mod, router_grad,
@@ -1785,7 +1786,7 @@
     ).astype(bf)
     router_grad[...] = tn(d_logits, second[...])
     d_second = (
-        d_shared[...] + nt(d_logits, router[...]) + (nn(hot[0], d_returned[...]) + nn(hot[1], d_returned[...]))
+        d_shared[...] + nn(d_logits, router_t[...].astype(bf)) + (nn(hot[0], d_returned[...]) + nn(hot[1], d_returned[...]))
     )
     normed, inv_std = layer_stats(residual[...])
     image_sums(3, d_second)
@@ -1882,6 +1883,46 @@
         compiler_params=pltpu.CompilerParams(vmem_limit_bytes=67043328),
         cost_estimate=pl.CostEstimate(flops=60_000_000_000, bytes_accessed=30_000_000, transcendentals=0),
         name="rear",
+    )(*operands)
+
+
+def last_kernel(
+    qkvo_sum, first, second, ada, up, down, d_act, router, condition,
+    qkv_out, out_out, first_out, second_out, ada_out, up_out, down_out, condition_out, router_out,
+):
+    d = lax.axis_index("dp")
+    qkv_out[...] = qkvo_sum[:, 0:576]
+    out_out[...] = qkvo_sum[:, 576:768]
+    first_out[...] = first[...]
+    second_out[...] = second[...]
+    ada_out[...] = ada[...]
+    up_out[...] = up[...]
+    down_out[...] = down[...]
+    router_out[...] = lines_of(router[...], 2 * d)[:, 0:96]
+    for f in range(8):
+        columns = slice(96 * f, 96 * f + 96)
+        v = condition[:, columns].astype(jnp.float32)
+        sigmoid = jax.nn.sigmoid(v)
+        condition_out[:, columns] = lines_of(d_act[f], 2 * d)[:, 0:96] * (
+            sigmoid * (1.0 + v * (1.0 - sigmoid))
+        )
+
+
+def last(*operands):
+    f32 = jnp.float32
+    return pl.pallas_call(
+        last_kernel,
+        out_shape=tuple(
+            jax.ShapeDtypeStruct(shape, f32)
+            for shape in (
+                (96, 576), (96, 192), (96, 768), (192, 384), (96, 1152), (2, 96, 3072), (2, 384, 768),
+                (2, 768), (2, 96),
+            )
+        ),
+        in_specs=[ONCHIP] * 9,
+        out_specs=(ONCHIP,) * 9,
+        compiler_params=pltpu.CompilerParams(vmem_limit_bytes=40 << 20),
+        name="last",
     )(*operands)
 
 
@@ -1920,26 +1961,16 @@
     act_slices = activated.astype(jnp.float32).reshape(IMG_DEV, 8, 96).transpose(1, 0, 2)
     act_slices = jnp.pad(act_slices, ((0, 0), (0, 6), (0, 32)))
     act_slices = act_slices.at[:, 2, :EXPERTS].set(counts)
-    ada_pad = jnp.pad(ada_weight, ((0, 32), (0, 0)))
-    router_pack = jnp.pad(router_weight.reshape(192), (0, 2048 - 192)).reshape(16, 128)
-    qkvo_shard = jnp.concatenate([qkv_weight, out_weight], axis=1)
-    qkvo, routers, seen, mod_rows, up_line, down_line, up_m, up_x0, up_y0, down_own, down_m = opening(
-        qkvo_shard, router_pack, act_slices, ada_pad, shared_up, shared_down.T, expert_up, expert_down
+    act_slices = act_slices.at[:, 3:5, :96].set(router_weight.T.astype(jnp.float32))
+    qkvo, router_t, seen, mod_rows, up_line, down_line, up_m, up_x0, up_y0, down_own, down_m = opening(
+        qkv_weight, out_weight, act_slices, ada_weight, shared_up, shared_down.T, expert_up, expert_down
     )
     hops = hop(up_m, 2), hop(up_m, 4), hop(down_own, 2), hop(down_own, 4)
     expert_counts = seen[66, :EXPERTS].astype(jnp.int32)
-    modulation = lax.dynamic_slice(mod_rows, (0, 2 * d_index, 0), (4, 2, 1152))
-    modulation = modulation.transpose(1, 0, 2).reshape(2, 4608)
-    router_full = (
-        routers.reshape(32, 2048)[:, :192]
-        .reshape(4, 8, 96, 2)
-        .transpose(1, 2, 0, 3)
-        .reshape(model_width, EXPERTS)
-    )
     segments = (segment[:, None], segment[None, :])
-    heads, totals, attended, projected, residual, second_input, d_mixed, gates, rows, grads = front(
-        tokens, modulation, inside, *segments, qkvo, router_full, cotangent, routes, target.T
-    )
+    (
+        heads, totals, attended, projected, residual, second_input, d_mixed, gates, rows, grads, modulation,
+    ) = front(tokens, mod_rows, inside, *segments, qkvo, router_t, cotangent, routes, target.T)
     rows = rows.reshape(EXPERTS, CAP, model_width)
     grads = grads.reshape(EXPERTS, CAP, model_width)
     rows, (up_x1, up_y1, down_x0, down_y0) = lax.optimization_barrier((rows, hops))
@@ -1958,7 +1989,7 @@
     returned = returned.reshape(EXPERTS * CAP, model_width)
     d_returned = d_returned.reshape(EXPERTS * CAP, model_width)
     output, tokens_grad, qkvo_grad, d_modulation, router_grad = rear(
-        tokens, modulation, inside, *segments, qkvo, router_full, cotangent, routes, target,
+        tokens, modulation, inside, *segments, qkvo, router_t, cotangent, routes, target,
         heads, totals, attended, projected, residual, second_input, gates,
         returned, d_returned, shared_out, d_second,
     )
@@ -1979,20 +2010,23 @@
         (d_mod_rows, router_tiles, seen[:64].astype(bf), ada_weight),
         (up_keep, *up_near, *up_next, down_keep, *down_near),
     )
-    d_activated = lax.dynamic_slice(d_act_tiles, (0, 2 * d_index, 0), (8, 2, 96))
-    d_activated = d_activated.transpose(1, 0, 2).reshape(2, model_width)
-    condition_grad = jax.vjp(jax.nn.silu, cond_float)[1](d_activated)[0]
-    router_out = lax.dynamic_slice(router_sum, (2 * d_index, 0), (2, 96)).T
+    (
+        qkv_grad, out_grad, shared_first_sum, shared_second_sum, ada_grad, expert_up_grad, expert_down_grad,
+        condition_grad, router_out,
+    ) = last(
+        qkvo_sum, shared_first_sum, shared_second_sum, ada_grad, expert_up_grad, expert_down_grad,
+        d_act_tiles, router_sum, condition,
+    )
     return (
         output,
         tokens_grad,
         condition_grad,
         ada_grad,
-        qkvo_sum[:, :576],
-        qkvo_sum[:, 576:],
+        qkv_grad,
+        out_grad,
         shared_first_sum,
         shared_second_sum.T,
-        router_out,
+        router_out.T,
         expert_up_grad,
         expert_down_grad,
         expert_counts,

time: 436 us -> 424 us (0.972)
  local copies, waits for them, and re-layouts: 29.8 us -> 17.2 us
    unnamed x31 -> x37, local copies, waits for them, and re-layouts: 13 us -> 11.8 us
  transfers between devices with their start and end apart: 8 -> 8, of which waited for: 0 -> 0; matrix products, arithmetic and copies ran while one was open for 3% -> 2% of each run, Pallas kernels for 18% -> 18%
where the time goes in v1:
time: 424 us; the launch traced here: 419 us
  Pallas kernels  382 us (90%)
  local copies, waits for them, and re-layouts  17.2 us (4%)
  other arithmetic  10.2 us (2%)
  starting transfers between devices  8.17 us (2%)
    pallas_call x1, Pallas kernels, experts(): pl.pallas_call(expert_kernel, out_shape=(jax.ShapeDtypeStruct((8, 144, 76...  102 us
    pallas_call x1, Pallas kernels, outbound(): pl.pallas_call(out_kernel, out_shape=(jax.ShapeDtypeStruct((8, 144, 768),...  88.9 us
    pallas_call x1, Pallas kernels, opening(): pl.pallas_call(open_kernel, out_shape=(jax.ShapeDtypeStruct((768, 3072),...  60.3 us
    pallas_call x1, Pallas kernels, dense_sums(): pl.pallas_call(dense_kernel, out_shape=(jax.ShapeDtypeStruct((96, 768), f...  52 us
    pallas_call x1, Pallas kernels, rear(): pl.pallas_call(rear_kernel, out_shape=(jax.ShapeDtypeStruct((512, 768), b...  43.4 us
    pallas_call x1, Pallas kernels, front(): pl.pallas_call(front_kernel, out_shape=(jax.ShapeDtypeStruct((36, 512, 64...  32.4 us
    unnamed x37, local copies, waits for them, and re-layouts  11.8 us
  transfers between devices with their start and end apart: 8, of which 0 were waited for; matrix products, arithmetic and copies ran while one was open for 2% of the time, Pallas kernels for 18%

profile of v1, /device:TPU:0, one launch (start us, length us, event | category | flops | bytes accessed | tf_op | source)
XLA Modules:
  0.0 418.5 jit_solution(10454322447250544806)
XLA Ops:
  0.6 0.8 reduce-window.8
  6.7 60.3 %opening.1 = (bf16[768,3072]{1,0:T(8,128)(2,1)}, f32[8,768]{1,0:T(8,128)}, f32[72,128]{1,0:T(8,128)}, f32[4,8,1152]{2,1,0:T(8,128)}, bf16[96,3072]{1,0:T(8,128)(...) custom-call(bf16[96,576]{1,0:T(8,128)(2,1)} %qkv_shard.1, ...), custom_call_target="tpu_custom_call" | custom-call | tf_op jit(solution)/shard_map/opening/pallas_call | solution.py:811
  67.0 1.4 collective-permute-start
  69.1 1.4 collective-permute-start.2
  71.4 0.9 copy.55.routes
  72.3 0.9 copy.54.seg_col
  73.8 32.4 %front.1 = (bf16[36,512,64]{2,1,0:T(8,128)(2,1)}, f32[12,512,1]{2,1,0:T(8,128)}, bf16[512,768]{1,0:T(8,128)(2,1)}, f32[512,768]{1,0:T(8,128)}, f32[512,768]{1,0:...) custom-call(bf16[512,768]{1,0:T(8,128)(2,1)} %tokens.3, ...), custom_call_target="tpu_custom_call" | custom-call | flops 40000000000 | bytes 20000000 | tf_op jit(solution)/shard_map/front/pallas_call | solution.py:1720
  106.1 0.9 copy.58.target
  107.0 1.4 slice.86.act
  108.3 1.2 convert_bitcast_fusion.2
  110.6 88.9 %outbound.1 = (bf16[8,144,768]{2,1,0:T(8,128)(2,1)}, bf16[8,144,768]{2,1,0:T(8,128)(2,1)}, bf16[2,96,3072]{2,1,0:T(8,128)(2,1)}, bf16[384,768]{1,0:T(8,128)(2,1)...) custom-call(bf16[8,144,768]{2,1,0:T(8,128)(2,1)} %bitcast.42, ...), custom_call_target="tpu_custom_call" | custom-call | tf_op jit(solution)/shard_map/outbound/pallas_call | solution.py:977
  199.5 102.0 %experts.1 = (bf16[8,144,768]{2,1,0:T(8,128)(2,1)}, bf16[8,144,768]{2,1,0:T(8,128)(2,1)}, bf16[2,2,96,3072]{3,2,1,0:T(8,128)(2,1)}, bf16[2,96,3072]{2,1,0:T(8,12...) custom-call(bf16[8,144,768]{2,1,0:T(8,128)(2,1)} %get-tuple-element., ...), custom_call_target="tpu_custom_call" | custom-call | tf_op jit(solution)/shard_map/experts/pallas_call | solution.py:1175
  301.5 3.0 fusion
  304.5 1.4 collective-permute-start.6
  306.5 1.4 collective-permute-start.4
  308.6 43.4 %rear.1 = (bf16[512,768]{1,0:T(8,128)(2,1)}, f32[512,768]{1,0:T(8,128)}, bf16[768,3072]{1,0:T(8,128)(2,1)}, f32[2,4608]{1,0:T(2,128)}, f32[8,768]{1,0:T(8,128)}) custom-call(bf16[512,768]{1,0:T(8,128)(2,1)} %tokens.3, f32[2,4608]{1,0:T(2,128)} %get-tuple-element.113.mod, f32[512,2]{1,0:T(8,128)} %get-tuple-element.188.inside, s32[512,1]{1,0:T(8,128)} %copy.54.seg_col, ...), custom_call_target="tpu_custom_call" | custom-call | flops 60000002048 | bytes 30000000 | tf_op jit(solution)/shard_map/rear/pallas_call | solution.py:1861
  354.9 52.0 %dense_sums.1 = (f32[96,768]{1,0:T(8,128)}, f32[96,768]{1,0:T(8,128)}, f32[192,384]{1,0:T(8,128)}, f32[96,1152]{1,0:T(8,128)}, f32[8,8,128]{2,1,0:T(8,128)}, /*i...) custom-call(bf16[768,3072]{1,0:T(8,128)(2,1)} %get-tuple-element.156.grad, ...), custom_call_target="tpu_custom_call" | custom-call | flops 40000000000 | bytes 20000000 | tf_op jit(solution)/shard_map/dense_sums/pallas_call | solution.py:1583
  406.9 1.7 copy-done
  408.6 1.7 copy-done.1
  410.2 1.0 copy-done.2
  411.3 1.0 copy-done.3
  412.2 1.0 copy-done.4
  413.2 1.0 copy-done.5
  415.6 2.7 last.1
  (66 shorter events, 14.0 us)
Async XLA Ops:
  5.2 67.0 %copy-start.17 = (s32[512]{0:T(512)}, s32[512]{0:T(512)S(1)}, u32[]{:S(2)}) copy-start(s32[512]{0:T(512)S(1)} %get-tuple-element.185) | copy-start | bytes 6148
  6.7 64.6 %copy-start.15 = (s32[512,2]{0,1:T(2,128)S(1)}, s32[512,2]{0,1:T(2,128)}, u32[]{:S(2)}) copy-start(s32[512,2]{0,1:T(2,128)} %param.27) | copy-start | bytes 12292
  67.0 42.5 %collective-permute-start = (bf16[96,3072]{1,0:T(8,128)(2,1)}, bf16[96,3072]{1,0:T(8,128)(2,1)S(1)}, u32[]{:S(2)}, u32[]{:S(2)}) collective-permute-start(bf16[96,3072]{1,0:T(8,128)(2,1)} %get-tuple-element.122.up_m), channel_id=1, source_target_pairs={{0,2},{1,3},{2,0},{3,1},{4,6},{5,7},{6,4},{7,5},{8,10},{9,11},{10,... | collective-permute-start | bytes 1769480 | tf_op jit(solution)/shard_map/ppermute | solution.py:1214
  68.4 41.1 %collective-permute-start.1 = (bf16[96,3072]{1,0:T(8,128)(2,1)}, bf16[96,3072]{1,0:T(8,128)(2,1)S(1)}, u32[]{:S(2)}, u32[]{:S(2)}) collective-permute-start(bf16[96,3072]{1,0:T(8,128)(2,1)} %get-tuple-element.122.up_m), channel_id=1, source_target_pairs={{0,4},{1,5},{2,6},{3,7},{4,0},{5,1},{6,2},{7,3},{8,12},{9,13},{10,... | collective-permute-start | bytes 1769480 | tf_op jit(solution)/shard_map/ppermute | solution.py:1214
  69.1 40.5 %collective-permute-start.2 = (bf16[384,768]{1,0:T(8,128)(2,1)}, bf16[384,768]{1,0:T(8,128)(2,1)S(1)}, u32[]{:S(2)}, u32[]{:S(2)}) collective-permute-start(bf16[384,768]{1,0:T(8,128)(2,1)} %get-tuple-element.123.down_own), channel_id=1, source_target_pairs={{0,2},{1,3},{2,0},{3,1},{4,6},{5,7},{6,4},{7,5},{8,10},{9,11},{10,... | collective-permute-start | bytes 1769480 | tf_op jit(solution)/shard_map/ppermute | solution.py:1214
  70.5 39.1 %collective-permute-start.3 = (bf16[384,768]{1,0:T(8,128)(2,1)}, bf16[384,768]{1,0:T(8,128)(2,1)S(1)}, u32[]{:S(2)}, u32[]{:S(2)}) collective-permute-start(bf16[384,768]{1,0:T(8,128)(2,1)} %get-tuple-element.123.down_own), channel_id=1, source_target_pairs={{0,4},{1,5},{2,6},{3,7},{4,0},{5,1},{6,2},{7,3},{8,12},{9,13},{10,... | collective-permute-start | bytes 1769480 | tf_op jit(solution)/shard_map/ppermute | solution.py:1214
  73.8 32.4 %copy-start.16 = (s32[512,2]{0,1:T(2,128)S(1)}, s32[512,2]{0,1:T(2,128)}, u32[]{:S(2)}) copy-start(s32[512,2]{0,1:T(2,128)} %convert_add_fusion.2) | copy-start | bytes 12292
  109.5 90.0 %copy-start.11 = (bf16[96,3072]{1,0:T(8,128)(2,1)}, bf16[96,3072]{1,0:T(8,128)(2,1)S(1)}, u32[]{:S(2)}) copy-start(bf16[96,3072]{1,0:T(8,128)(2,1)S(1)} %collective-permute-done.up_x1) | copy-start | bytes 1769476
  109.5 0.8 copy-start.9
  109.6 1.0 copy-start.10
  109.6 89.9 %copy-start.12 = (bf16[384,768]{1,0:T(8,128)(2,1)}, bf16[384,768]{1,0:T(8,128)(2,1)S(1)}, u32[]{:S(2)}) copy-start(bf16[384,768]{1,0:T(8,128)(2,1)S(1)} %collective-permute-done.3.down_y0) | copy-start | bytes 1769476
  304.5 49.7 %collective-permute-start.6 = (bf16[96,3072]{1,0:T(8,128)(2,1)}, bf16[96,3072]{1,0:T(8,128)(2,1)}, u32[]{:S(2)}, u32[]{:S(2)}) collective-permute-start(bf16[96,3072]{1,0:T(8,128)(2,1)} %get-tuple-element.187), channel_id=1, source_target_pairs={{0,4},{1,5},{2,6},{3,7},{4,0},{5,1},{6,2},{7,3},{8,12},{9,13},{10,... | collective-permute-start | bytes 1769480 | tf_op jit(solution)/shard_map/ppermute | solution.py:1214
  305.9 48.4 %collective-permute-start.7 = (bf16[96,3072]{1,0:T(8,128)(2,1)}, bf16[96,3072]{1,0:T(8,128)(2,1)}, u32[]{:S(2)}, u32[]{:S(2)}) collective-permute-start(bf16[96,3072]{1,0:T(8,128)(2,1)} %get-tuple-element.186), channel_id=1, source_target_pairs={{0,2},{1,3},{2,0},{3,1},{4,6},{5,7},{6,4},{7,5},{8,10},{9,11},{10,... | collective-permute-start | bytes 1769480 | tf_op jit(solution)/shard_map/ppermute | solution.py:1214
  306.5 47.7 %collective-permute-start.4 = (bf16[2,384,768]{2,1,0:T(8,128)(2,1)}, bf16[2,384,768]{2,1,0:T(8,128)(2,1)}, u32[]{:S(2)}, u32[]{:S(2)}) collective-permute-start(bf16[2,384,768]{2,1,0:T(8,128)(2,1)} %get-tuple-element.151), channel_id=1, source_target_pairs={{0,2},{1,3},{2,0},{3,1},{4,6},{5,7},{6,4},{7,5},{8,10},{9,11},{10,... | collective-permute-start | bytes 3538952 | tf_op jit(solution)/shard_map/ppermute | solution.py:1214
  307.9 46.4 %collective-permute-start.5 = (bf16[2,384,768]{2,1,0:T(8,128)(2,1)}, bf16[2,384,768]{2,1,0:T(8,128)(2,1)}, u32[]{:S(2)}, u32[]{:S(2)}) collective-permute-start(bf16[2,384,768]{2,1,0:T(8,128)(2,1)} %get-tuple-element.152), channel_id=1, source_target_pairs={{0,4},{1,5},{2,6},{3,7},{4,0},{5,1},{6,2},{7,3},{8,12},{9,13},{10,... | collective-permute-start | bytes 3538952 | tf_op jit(solution)/shard_map/ppermute | solution.py:1214
  354.9 52.0 %copy-start.7 = (bf16[2,768]{1,0:T(2,128)(2,1)S(1)}, bf16[2,768]{1,0:T(2,128)(2,1)}, u32[]{:S(2)}) copy-start(bf16[2,768]{1,0:T(2,128)(2,1)} %condition.1) | copy-start | bytes 9220
  406.9 1.7 copy-start
  408.6 1.7 copy-start.1
  410.2 1.0 copy-start.2
  411.3 1.0 copy-start.3
  412.2 1.0 copy-start.4
  413.2 1.0 copy-start.5
  414.1 0.8 copy-start.6
  414.9 0.7 copy-start.8
  (2 other events, 1.3 us)
